TPU v7x, 256 devices: a whole 4x4x8 slice. The times are simulated.
256 devices in a mesh: dp: 4 (over x), mp: 64 (over z, y, core).
Axes of the slice: x: 4, y: 4, z: 8, core: 2. Of those that a mesh axis runs over, the one named last changes fastest.
Arguments:
- residual: bfloat16 [1024, 4096], P(('dp', 'mp')), may hold values from -6 to 6
- ffn_gain: float32 [4096], replicated, may hold values from 0.5 to 1.5
- gate_weight: bfloat16 [4096, 8192], P(None, 'mp'), may hold values from -0.09375 to 0.09375
- up_weight: bfloat16 [4096, 8192], P(None, 'mp'), may hold values from -0.09375 to 0.09375
- down_weight: bfloat16 [8192, 4096], P('mp'), may hold values from -0.0625 to 0.0625
- final_gain: float32 [4096], replicated, may hold values from 0.5 to 1.5
- head_weight: bfloat16 [4096, 65536], P(None, 'mp')
- passage_ids: int32 [4, 256], P('dp'), may hold values from 0 to 3, never falling along the last dimension, each value on 1 to 128 neighbouring positions
- valid_counts: int32 [4, 4], P('dp'), may hold values from 1 to 128
Outputs:
- term_weights: float32 [16, 65536], P('dp', 'mp')
- entropy: float32 [], replicated
- grad_hidden: float32 [1024, 4096], P(('dp', 'mp'))
Inputs may be any that keep to these rules, and one draw needn't show every extreme that they name: `passage_ids`: within each group the ids never fall and every passage of 0 to 3 has 1 to 128 rows.
All inputs are finite; a program needn't handle non-finite values.
Results may differ from a plain program's by a relative error of at most 0.0069.
The roundings to bfloat16 on the way count: a program that leaves them out, or rounds other values in their place, can miss the bound.
Values may be sent and summed in bfloat16 or wider, within the bound.
No kernel may reach another device: no remote copies, remote signals or barrier semaphores. Data moves between devices by JAX's collectives and lax.ppermute only.
A program may use at most 64 MiB of HBM per device.

v0:
```python
import jax
import jax.numpy as jnp
from jax import lax
from jax.sharding import Mesh, PartitionSpec as P


PLANE = ("z", "y")
ALL = ("dp", "z", "y", "c")
MP = ("z", "y", "c")
BF = jnp.bfloat16
F32 = jnp.float32


def rms_scale(values):
    return lax.rsqrt(jnp.mean(values * values, axis=-1, keepdims=True) + 1e-05)


def pool_masks(ids, counts):
    slots = jnp.arange(counts.shape[0], dtype=jnp.int32)
    member = ids[:, None] == slots[None, :]
    starts = jnp.sum((ids[:, None] < slots[None, :]).astype(jnp.int32), axis=0)
    start_row = jnp.sum(jnp.where(member, starts[None, :], 0), axis=1)
    count_row = jnp.sum(jnp.where(member, counts[None, :], 0), axis=1)
    position = jnp.arange(ids.shape[0], dtype=jnp.int32) - start_row
    valid = (position < count_row).astype(F32)
    return (member.astype(F32), valid)


def swap(x):
    return lax.ppermute(x, "c", [(0, 1), (1, 0)])


def mm(a, b):
    return jnp.dot(a, b, preferred_element_type=F32)


def mm_t(a, b):
    return lax.dot_general(a, b, (((1,), (1,)), ((), ())), preferred_element_type=F32)


def halves(x, core, axis):
    size = x.shape[axis] // 2
    own = lax.dynamic_slice_in_dim(x, core * size, size, axis)
    other = lax.dynamic_slice_in_dim(x, (1 - core) * size, size, axis)
    return own, other


def chip_rows(x, core):
    own, other = halves(x, core, 1)
    got = swap(other)
    return jnp.where(core == 0, jnp.concatenate([own, got], 0), jnp.concatenate([got, own], 0))


def core_rows(x, core):
    own, other = halves(x, core, 0)
    got = swap(other)
    return jnp.where(core == 0, jnp.concatenate([own, got], 1), jnp.concatenate([got, own], 1))


def exchange(x, axes):
    return lax.all_to_all(x, axes, 0, 0)


def gather(block, n):
    spread = jnp.broadcast_to(block[None], (n, *block.shape))
    mine = exchange(spread, PLANE).reshape(-1, block.shape[-1])
    return mine, swap(mine)


def scatter(own, other, n):
    both = (own + swap(other).astype(F32)).astype(BF)
    moved = exchange(both.reshape(n, -1, both.shape[-1]), PLANE)
    return jnp.sum(moved.astype(F32), axis=0)


def body(
    residual,
    ffn_gain,
    gate_weight,
    up_weight,
    down_weight,
    final_gain,
    head_weight,
    passage_ids,
    valid_counts,
):
    highest = lax.Precision.HIGHEST
    core = lax.axis_index("c")
    n = lax.axis_size(PLANE)
    n_dp = lax.axis_size("dp")
    n_mp = lax.axis_size(MP)
    own_rows = residual.astype(F32)
    normed_in = (own_rows * rms_scale(own_rows) * ffn_gain).astype(BF)
    member, valid = pool_masks(passage_ids[0], valid_counts[0])
    gate_up = jnp.concatenate([gate_weight, up_weight], axis=1)
    mine, theirs = gather(chip_rows(normed_in, core), n)
    residual8 = chip_rows(residual, core).astype(F32)
    gain8 = halves(final_gain[None, :], core, 1)[0]

    gu_own, gu_other = halves(gate_up, core, 0)
    gu = mm(mine, gu_own) + mm(theirs, gu_other)
    hid = gate_weight.shape[1]
    activated = (jax.nn.silu(gu[:, :hid]) * gu[:, hid:]).astype(BF)
    down_own, down_other = halves(down_weight, core, 1)
    other = mm(activated, down_other).astype(BF)
    hidden8 = residual8 + scatter(mm(activated, down_own), other, n)
    square = jnp.sum(hidden8 * hidden8, axis=1, keepdims=True)
    width = residual.shape[1]
    scale8 = lax.rsqrt((square + swap(square)) / width + 1e-05)
    normed8 = (hidden8 * scale8 * gain8).astype(BF)
    mine, theirs = gather(normed8, n)
    hidden = core_rows(hidden8, core)
    scale = rms_scale(hidden)

    head_own, head_other = halves(head_weight, core, 0)
    logits = mm(mine, head_own) + mm(theirs, head_other)
    positive = jnp.maximum(logits, 0.0)
    weights = jnp.log1p(positive)
    powered = valid[:, None] * weights**4
    pooled_sum = lax.dot_general(member, powered, (((0,), (0,)), ((), ())), precision=highest)
    term_weights = (1.0 + pooled_sum) ** 0.25 - 1.0
    local_mass = jnp.sum(term_weights, axis=0).reshape(1, -1, 128)
    masses = exchange(jnp.broadcast_to(local_mass, (n_dp, *local_mass.shape[1:])), "dp")
    slope = lax.optimization_barrier(valid[:, None] * weights**3 / (1.0 + positive))
    smooth = 1.0 + jnp.sum(masses, axis=0).reshape(-1)
    log_smooth = jnp.log(smooth)
    lane = jnp.arange(128)
    sums = jnp.where(lane == 0, jnp.sum(smooth), jnp.where(lane == 1, jnp.sum(smooth * log_smooth), 0.0))
    sums = exchange(jnp.broadcast_to(sums, (n_mp, 1, 128)), MP)
    row_factor = jnp.dot(member, (1.0 + pooled_sum) ** (-0.75), precision=highest)
    slope = lax.optimization_barrier(slope * row_factor)
    sums = jnp.sum(sums, axis=(0, 1))
    total, spread = sums[0], sums[1]
    entropy = jnp.log(total) - spread / total
    slope_mass = jnp.log(total) - log_smooth
    slope_logit = lax.optimization_barrier((slope * slope_mass[None, :]).astype(BF))
    other = mm_t(slope_logit, head_other).astype(BF)
    slope_normed = core_rows(scatter(mm_t(slope_logit, head_own), other, n), core)
    scaled_slope = slope_normed * final_gain
    grad_hidden = scale * scaled_slope - hidden * scale**3 * jnp.mean(
        scaled_slope * hidden, axis=-1, keepdims=True
    )
    return (term_weights, entropy, grad_hidden)


def solution(mesh):
    axes = Mesh(mesh.devices.reshape(mesh.shape["dp"], 8, 4, 2), ALL)
    placed = (
        P(ALL, None),
        P(),
        P(None, MP),
        P(None, MP),
        P(MP, None),
        P(),
        P(None, MP),
        P("dp", None),
        P("dp", None),
    )
    return jax.shard_map(
        body,
        mesh=axes,
        in_specs=placed,
        out_specs=(P("dp", MP), P(), P(ALL, None)),
        check_vma=False,
    )
```

profile of v0, /device:TPU:2, one launch (start us, length us, event | category | flops | bytes accessed | tf_op | source)
XLA Modules:
  0.0 207.0 jit_solution(15682096092013070548)
XLA Ops:
  0.7 1.1 fusion.34
  1.7 0.9 fusion.36
  2.7 1.2 collective-permute-done.1
  4.0 39.8 %all_to_all.30 = bf16[32,8,2048]{2,1,0:T(8,128)(2,1)S(1)} all-to-all(bf16[32,8,2048]{2,1,0:T(8,128)(2,1)S(1)} %broadcast_in_dim.73), channel_id=1, replica_groups=mesh['dp'=4,'z'=8,'y'=4,'c'=2] {'z','y'}, dimensions={0} | all-to-all | bytes 2097152 | tf_op jit(solution)/shard_map/all_to_all | solution.py:61
  44.3 0.4 fusion.24
  44.7 1.7 collective-permute-done.2
  46.5 0.4 convolution_add_fusion
  47.7 2.5 %collective-permute-done.3 = bf16[256,2048]{1,0:T(8,128)(2,1)S(1)} collective-permute-done((bf16[256,2048]{1,0:T(8,128)(2,1)S(1)}, bf16[256,2048]{1,0:T(8,128)(2,1)S(1)}, u32[]{:S(2)}, u32[]{:S(2)}) %collective-permute-start.3) | collective-permute-done | bytes 1048608 | tf_op jit(solution)/shard_map/ppermute | solution.py:30
  50.2 1.4 fusion.21
  51.6 5.7 %all-to-all-start.1 = ((bf16[32,8,2048]{2,1,0:T(8,128)(2,1)}), bf16[32,8,2048]{2,1,0:T(8,128)(2,1)S(1)}, u32[]{:S(2)}, u32[]{:S(2)}) async-start(bf16[32,8,2048]{2,1,0:T(8,128)(2,1)} %fusion.21), calls=%async_computation.1 | async-start | bytes 2097152 | tf_op jit(solution)/shard_map/all_to_all | solution.py:61
  57.5 28.2 %all-to-all-done.1 = bf16[32,8,2048]{2,1,0:T(8,128)(2,1)S(1)} async-done(((bf16[32,8,2048]{2,1,0:T(8,128)(2,1)}), bf16[32,8,2048]{2,1,0:T(8,128)(2,1)S(1)}, u32[]{:S(2)}, u32[]{:S(2)}) %all-to-all-start.1) | async-done | bytes 1048608 | tf_op jit(solution)/shard_map/all_to_all | solution.py:61
  86.1 1.1 collective-permute-done.4
  87.5 33.8 %all_to_all.31 = bf16[32,8,2048]{2,1,0:T(8,128)(2,1)S(1)} all-to-all(bf16[32,8,2048]{2,1,0:T(8,128)(2,1)S(1)} %broadcast_in_dim.75), channel_id=1, replica_groups=mesh['dp'=4,'z'=8,'y'=4,'c'=2] {'z','y'}, dimensions={0} | all-to-all | bytes 2097152 | tf_op jit(solution)/shard_map/all_to_all | solution.py:61
  121.4 3.5 %fusion.6 = f32[256,1024]{1,0:T(8,128)S(1)} fusion(bf16[4096,1024]{1,0:T(8,128)(2,1)} %param.15, s32[]{:T(128)} %select_n.73, bf16[32,8,2048]{2,1,0:T(8,128)(2,1)S(1)} %all_to_all.31), kind=kOutput, calls=%fused_computation.6 | convolution fusion | flops 1073741824 | bytes 6291968 | tf_op jit(solution)/shard_map/dot_general | solution.py:34
  124.9 3.9 %fusion.20 = (f32[256,1024]{1,0:T(8,128)S(1)}, f32[256,1024]{1,0:T(8,128)S(1)}) fusion(f32[256]{0:T(256)S(1)} %compare_convert_fusion, f32[256,1024]{1,0:T(8,128)S(1)} %fusion.6, bf16[256,2048]{1,0:T(8,128)(2,1)S(1)} %collective-permute-done.5, bf16[4096,1024]{1,0:T(8,128)(2,1)} %param.15, s32[]{:T(128)S(6)} %select_n.74), kind=kOutput, calls=%fused_computation.23 | convolution fusion | flops 1075576832 | bytes 8389636 | tf_op jit(solution)/shard_map/dot_general | solution.py:34
  128.8 1.5 fusion.57
  130.3 0.6 broadcast_in_dim.77
  130.9 4.8 %all-to-all-start.3 = ((f32[4,8,128]{2,1,0:T(8,128)}), f32[4,8,128]{2,1,0:T(8,128)S(1)}, u32[]{:S(2)}, u32[]{:S(2)}) async-start(f32[4,8,128]{2,1,0:T(8,128)} %broadcast_in_dim.77), calls=%async_computation.3 | async-start | bytes 32768 | tf_op jit(solution)/shard_map/all_to_all | solution.py:61
  135.8 3.9 %all-to-all-done.3 = f32[4,8,128]{2,1,0:T(8,128)S(1)} async-done(((f32[4,8,128]{2,1,0:T(8,128)}), f32[4,8,128]{2,1,0:T(8,128)S(1)}, u32[]{:S(2)}, u32[]{:S(2)}) %all-to-all-start.3) | async-done | bytes 16416 | tf_op jit(solution)/shard_map/all_to_all | solution.py:61
  139.7 0.7 add_reduce_fusion
  140.4 1.3 compare_select_fusion.1
  141.7 0.6 broadcast_in_dim.81
  142.3 6.4 %all-to-all-start.4 = ((f32[64,1,128]{2,1,0:T(1,128)}), f32[64,1,128]{2,1,0:T(1,128)S(1)}, u32[]{:S(2)}, u32[]{:S(2)}) async-start(f32[64,1,128]{2,1,0:T(1,128)} %broadcast_in_dim.81), calls=%async_computation.4 | async-start | bytes 65536 | tf_op jit(solution)/shard_map/all_to_all | solution.py:61
  148.7 0.6 convolution_multiply_fusion
  149.4 8.7 %all-to-all-done.4 = f32[64,1,128]{2,1,0:T(1,128)S(1)} async-done(((f32[64,1,128]{2,1,0:T(1,128)}), f32[64,1,128]{2,1,0:T(1,128)S(1)}, u32[]{:S(2)}, u32[]{:S(2)}) %all-to-all-start.4) | async-done | bytes 32800 | tf_op jit(solution)/shard_map/all_to_all | solution.py:61
  158.1 0.6 fusion.58
  159.6 3.5 %fusion.8 = bf16[256,2048]{1,0:T(8,128)(2,1)S(1)} fusion(bf16[256,1024]{1,0:T(8,128)(2,1)S(1)} %multiply_convert_fusion, bf16[4096,1024]{1,0:T(8,128)(2,1)} %param.15, s32[]{:T(128)S(6)} %select_n.74), kind=kOutput, calls=%fused_computation.8 | convolution fusion | flops 1074266112 | bytes 5767172 | tf_op jit(solution)/shard_map/dot_general | solution.py:38
  163.2 2.6 %collective-permute-done.7 = bf16[256,2048]{1,0:T(8,128)(2,1)S(1)} collective-permute-done((bf16[256,2048]{1,0:T(8,128)(2,1)S(1)}, bf16[256,2048]{1,0:T(8,128)(2,1)S(1)}, u32[]{:S(2)}, u32[]{:S(2)}) %collective-permute-start.7) | collective-permute-done | bytes 1048608 | tf_op jit(solution)/shard_map/ppermute | solution.py:30
  165.8 4.5 %fusion.22 = bf16[32,8,2048]{2,1,0:T(8,128)(2,1)} fusion(bf16[256,2048]{1,0:T(8,128)(2,1)S(1)} %collective-permute-done.7, bf16[256,1024]{1,0:T(8,128)(2,1)S(1)} %multiply_convert_fusion, bf16[4096,1024]{1,0:T(8,128)(2,1)} %param.15, s32[]{:T(128)} %select_n.73), kind=kOutput, calls=%fused_computation.25 | convolution fusion | flops 1075314688 | bytes 6816256 | tf_op jit(solution)/shard_map/dot_general | solution.py:38
  170.3 4.1 %all-to-all-start.5 = ((bf16[32,8,2048]{2,1,0:T(8,128)(2,1)}), bf16[32,8,2048]{2,1,0:T(8,128)(2,1)S(1)}, u32[]{:S(2)}, u32[]{:S(2)}) async-start(bf16[32,8,2048]{2,1,0:T(8,128)(2,1)} %fusion.22), calls=%async_computation.5 | async-start | bytes 2097152 | tf_op jit(solution)/shard_map/all_to_all | solution.py:61
  174.6 28.7 %all-to-all-done.5 = bf16[32,8,2048]{2,1,0:T(8,128)(2,1)S(1)} async-done(((bf16[32,8,2048]{2,1,0:T(8,128)(2,1)}), bf16[32,8,2048]{2,1,0:T(8,128)(2,1)S(1)}, u32[]{:S(2)}, u32[]{:S(2)}) %all-to-all-start.5) | async-done | bytes 1048608 | tf_op jit(solution)/shard_map/all_to_all | solution.py:61
  205.2 0.7 multiply_subtract_fusion
  (55 shorter events, 3.3 us)
Async XLA Ops:
  0.6 46.4 %copy-start = (bf16[128,4096]{1,0:T(8,128)(2,1)S(1)}, bf16[128,4096]{1,0:T(8,128)(2,1)}, u32[]{:S(2)}) copy-start(bf16[128,4096]{1,0:T(8,128)(2,1)} %param.13) | copy-start | bytes 3145732
  0.6 43.2 %copy-start.1 = (bf16[4096,128]{1,0:T(8,128)(2,1)S(1)}, bf16[4096,128]{1,0:T(8,128)(2,1)}, u32[]{:S(2)}) copy-start(bf16[4096,128]{1,0:T(8,128)(2,1)} %param.11) | copy-start | bytes 3145732
  2.6 1.3 collective-permute-start.1
  4.0 40.0 %copy-start.2 = (bf16[4096,128]{1,0:T(8,128)(2,1)S(1)}, bf16[4096,128]{1,0:T(8,128)(2,1)}, u32[]{:S(2)}) copy-start(bf16[4096,128]{1,0:T(8,128)(2,1)} %param.12) | copy-start | bytes 3145732
  43.8 2.7 %collective-permute-start.2 = (bf16[256,2048]{1,0:T(8,128)(2,1)S(1)}, bf16[256,2048]{1,0:T(8,128)(2,1)S(1)}, u32[]{:S(2)}, u32[]{:S(2)}) collective-permute-start(bf16[256,2048]{1,0:T(8,128)(2,1)S(1)} %bitcast.28), channel_id=1, source_target_pairs={{0,1},{1,0},{2,3},{3,2},{4,5},{5,4},{6,7},{7,6},{8,9},{9,8},{10,11... | collective-permute-start | bytes 3145736 | tf_op jit(solution)/shard_map/ppermute | solution.py:30
  47.4 9.9 %copy-start.3 = (bf16[4,4096]{1,0:T(4,128)(2,1)S(1)}, bf16[4,4096]{1,0:T(4,128)(2,1)}, u32[]{:S(2)}) copy-start(bf16[4,4096]{1,0:T(4,128)(2,1)} %param.9) | copy-start | bytes 98308
  47.5 2.7 %collective-permute-start.3 = (bf16[256,2048]{1,0:T(8,128)(2,1)S(1)}, bf16[256,2048]{1,0:T(8,128)(2,1)S(1)}, u32[]{:S(2)}, u32[]{:S(2)}) collective-permute-start(bf16[256,2048]{1,0:T(8,128)(2,1)S(1)} %convolution_convert_fusion), channel_id=1, source_target_pairs={{0,1},{1,0},{2,3},{3,2},{4,5},{5,4},{6,7},{7,6},{8,9},{9,8},{10,11... | collective-permute-start | bytes 3145736 | tf_op jit(solution)/shard_map/ppermute | solution.py:30
  51.6 35.6 %dynamic-slice-start = ((f32[4096]{0:T(1024)}, s32[]{:T(128)}), f32[2048]{0:T(1024)S(1)}, s32[]{:S(2)}) async-start(f32[4096]{0:T(1024)} %param.14, s32[]{:T(128)} %select_n.73), calls=%async_computation.6 | async-start | bytes 16896 | tf_op jit(solution)/shard_map/dynamic-slice
  51.6 34.1 %all-to-all-start.1 = ((bf16[32,8,2048]{2,1,0:T(8,128)(2,1)}), bf16[32,8,2048]{2,1,0:T(8,128)(2,1)S(1)}, u32[]{:S(2)}, u32[]{:S(2)}) async-start(bf16[32,8,2048]{2,1,0:T(8,128)(2,1)} %fusion.21), calls=%async_computation.1 | async-start | bytes 2097152 | tf_op jit(solution)/shard_map/all_to_all | solution.py:61
  57.4 28.5 %collective-permute-start = (bf16[4,2048]{1,0:T(4,128)(2,1)S(1)}, bf16[4,2048]{1,0:T(4,128)(2,1)S(1)}, u32[]{:S(2)}, u32[]{:S(2)}) collective-permute-start(bf16[4,2048]{1,0:T(4,128)(2,1)S(1)} %get-tuple-element.17), channel_id=1, source_target_pairs={{0,1},{1,0},{2,3},{3,2},{4,5},{5,4},{6,7},{7,6},{8,9},{9,8},{10,11... | collective-permute-start | bytes 49160 | tf_op jit(solution)/shard_map/ppermute | solution.py:30
  57.5 63.7 %copy-start.5 = (s32[1,256]{1,0:T(1,128)S(1)}, s32[1,256]{1,0:T(1,128)}, u32[]{:S(2)}) copy-start(s32[1,256]{1,0:T(1,128)} %param.16) | copy-start | bytes 3076
  57.5 63.8 %copy-start.6 = (s32[1,4]{1,0:T(1,128)S(1)}, s32[1,4]{1,0:T(1,128)}, u32[]{:S(2)}) copy-start(s32[1,4]{1,0:T(1,128)} %param.17) | copy-start | bytes 52
  86.0 1.2 collective-permute-start.4
  121.2 3.7 %collective-permute-start.5 = (bf16[256,2048]{1,0:T(8,128)(2,1)S(1)}, bf16[256,2048]{1,0:T(8,128)(2,1)S(1)}, u32[]{:S(2)}, u32[]{:S(2)}) collective-permute-start(bf16[256,2048]{1,0:T(8,128)(2,1)S(1)} %bitcast.29), channel_id=1, source_target_pairs={{0,1},{1,0},{2,3},{3,2},{4,5},{5,4},{6,7},{7,6},{8,9},{9,8},{10,11... | collective-permute-start | bytes 3145736 | tf_op jit(solution)/shard_map/ppermute | solution.py:30
  130.9 8.7 %all-to-all-start.3 = ((f32[4,8,128]{2,1,0:T(8,128)}), f32[4,8,128]{2,1,0:T(8,128)S(1)}, u32[]{:S(2)}, u32[]{:S(2)}) async-start(f32[4,8,128]{2,1,0:T(8,128)} %broadcast_in_dim.77), calls=%async_computation.3 | async-start | bytes 32768 | tf_op jit(solution)/shard_map/all_to_all | solution.py:61
  142.3 15.8 %all-to-all-start.4 = ((f32[64,1,128]{2,1,0:T(1,128)}), f32[64,1,128]{2,1,0:T(1,128)S(1)}, u32[]{:S(2)}, u32[]{:S(2)}) async-start(f32[64,1,128]{2,1,0:T(1,128)} %broadcast_in_dim.81), calls=%async_computation.4 | async-start | bytes 65536 | tf_op jit(solution)/shard_map/all_to_all | solution.py:61
  163.1 2.7 %collective-permute-start.7 = (bf16[256,2048]{1,0:T(8,128)(2,1)S(1)}, bf16[256,2048]{1,0:T(8,128)(2,1)S(1)}, u32[]{:S(2)}, u32[]{:S(2)}) collective-permute-start(bf16[256,2048]{1,0:T(8,128)(2,1)S(1)} %fusion.8), channel_id=1, source_target_pairs={{0,1},{1,0},{2,3},{3,2},{4,5},{5,4},{6,7},{7,6},{8,9},{9,8},{10,11... | collective-permute-start | bytes 3145736 | tf_op jit(solution)/shard_map/ppermute | solution.py:30
  170.3 34.7 %copy-start.4 = (f32[4096]{0:T(1024)S(1)}, f32[4096]{0:T(1024)}, u32[]{:S(2)}) copy-start(f32[4096]{0:T(1024)} %param.14) | copy-start | bytes 49156
  170.3 33.0 %all-to-all-start.5 = ((bf16[32,8,2048]{2,1,0:T(8,128)(2,1)}), bf16[32,8,2048]{2,1,0:T(8,128)(2,1)S(1)}, u32[]{:S(2)}, u32[]{:S(2)}) async-start(bf16[32,8,2048]{2,1,0:T(8,128)(2,1)} %fusion.22), calls=%async_computation.5 | async-start | bytes 2097152 | tf_op jit(solution)/shard_map/all_to_all | solution.py:61
  174.4 30.6 %collective-permute-start.6 = (f32[4,2048]{1,0:T(4,128)S(1)}, f32[4,2048]{1,0:T(4,128)S(1)}, u32[]{:S(2)}, u32[]{:S(2)}) collective-permute-start(f32[4,2048]{1,0:T(4,128)S(1)} %get-tuple-element.15), channel_id=1, source_target_pairs={{0,1},{1,0},{2,3},{3,2},{4,5},{5,4},{6,7},{7,6},{8,9},{9,8},{10,11... | collective-permute-start | bytes 98312 | tf_op jit(solution)/shard_map/ppermute | solution.py:30
  203.5 1.5 collective-permute-start.8
where the time goes:
time: 210 us; the launch traced here: 207 us
  waiting for transfers between devices  78.7 us (37%)
  blocking collectives  73.6 us (35%)
  starting transfers between devices  21.9 us (10%)
  matrix products  20.2 us (10%)
  other arithmetic  5.82 us (3%)
  between operations  4.24 us (2%)
  local copies, waits for them, and re-layouts  2.61 us (1%)
    all_to_all x2, blocking collectives, exchange(): return lax.all_to_all(x, axes, 0, 0)  73.6 us
    all_to_all x4, waiting for transfers between devices, exchange(): return lax.all_to_all(x, axes, 0, 0)  69.5 us
    all_to_all x4, starting transfers between devices, exchange(): return lax.all_to_all(x, axes, 0, 0)  21 us
    dot_general x6, matrix products, mm(): return jnp.dot(a, b, preferred_element_type=F32)  10.1 us
    ppermute x9, waiting for transfers between devices, swap(): return lax.ppermute(x, 'c', [(0, 1), (1, 0)])  9.24 us
    dot_general x2, matrix products, mm_t(): lax.dot_general(a, b, (((1,), (1,)), ((), ())), preferred_element_type=F32)  7.94 us
  transfers between devices with their start and end apart: 13, of which 9 were waited for; matrix products, arithmetic and copies ran while one was open for 3% of the time, Pallas kernels for 0%

commit v1 on v0

--- a/solution.py
+++ b/solution.py
@@ -68,7 +68,8 @@
 
 
 def scatter(own, other, n):
-    both = (own + swap(other).astype(F32)).astype(BF)
+    got = swap(other)
+    both = (own + got.astype(F32)).astype(BF)
     moved = exchange(both.reshape(n, -1, both.shape[-1]), PLANE)
     return jnp.sum(moved.astype(F32), axis=0)
 
@@ -119,23 +120,26 @@
     powered = valid[:, None] * weights**4
     pooled_sum = lax.dot_general(member, powered, (((0,), (0,)), ((), ())), precision=highest)
     term_weights = (1.0 + pooled_sum) ** 0.25 - 1.0
-    local_mass = jnp.sum(term_weights, axis=0).reshape(1, -1, 128)
-    masses = exchange(jnp.broadcast_to(local_mass, (n_dp, *local_mass.shape[1:])), "dp")
+    local_mass = jnp.sum(term_weights, axis=0).reshape(-1, 128)
+    first, second, third = (
+        lax.ppermute(local_mass, "dp", [(i, (i + k) % n_dp) for i in range(n_dp)])
+        for k in range(1, n_dp)
+    )
+    smooth = 1.0 + ((local_mass + second) + (first + third))
+    log_smooth = jnp.log(smooth)
+    sums = jnp.stack([jnp.sum(smooth, axis=0), jnp.sum(smooth * log_smooth, axis=0)])
+    sums = exchange(jnp.broadcast_to(sums[None], (n_mp, 2, 128)), MP)
     slope = lax.optimization_barrier(valid[:, None] * weights**3 / (1.0 + positive))
-    smooth = 1.0 + jnp.sum(masses, axis=0).reshape(-1)
-    log_smooth = jnp.log(smooth)
-    lane = jnp.arange(128)
-    sums = jnp.where(lane == 0, jnp.sum(smooth), jnp.where(lane == 1, jnp.sum(smooth * log_smooth), 0.0))
-    sums = exchange(jnp.broadcast_to(sums, (n_mp, 1, 128)), MP)
     row_factor = jnp.dot(member, (1.0 + pooled_sum) ** (-0.75), precision=highest)
     slope = lax.optimization_barrier(slope * row_factor)
-    sums = jnp.sum(sums, axis=(0, 1))
+    sums = jnp.sum(jnp.sum(sums, axis=0), axis=1)
     total, spread = sums[0], sums[1]
     entropy = jnp.log(total) - spread / total
-    slope_mass = jnp.log(total) - log_smooth
+    slope_mass = jnp.log(total) - log_smooth.reshape(-1)
     slope_logit = lax.optimization_barrier((slope * slope_mass[None, :]).astype(BF))
     other = mm_t(slope_logit, head_other).astype(BF)
-    slope_normed = core_rows(scatter(mm_t(slope_logit, head_own), other, n), core)
+    own = lax.optimization_barrier(mm_t(slope_logit, head_own))
+    slope_normed = core_rows(scatter(own, other, n), core)
     scaled_slope = slope_normed * final_gain
     grad_hidden = scale * scaled_slope - hidden * scale**3 * jnp.mean(
         scaled_slope * hidden, axis=-1, keepdims=True

time: 210 us -> 205 us (0.976)
  waiting for transfers between devices: 78.7 us -> 75.8 us
    all_to_all x4 -> x3, starting transfers between devices: 21 us -> 16 us  [exchange(): return lax.all_to_all(x, axes, 0, 0)]
    ppermute x0 -> x3, starting transfers between devices: none -> 4.15 us  [body(): lax.ppermute(local_mass, 'dp', [(i, (i + k) % n_dp) for i in range(n_dp)])]
    all_to_all x4 -> x3, waiting for transfers between devices: 69.5 us -> 66.3 us  [exchange(): return lax.all_to_all(x, axes, 0, 0)]
    ppermute x0 -> x3, waiting for transfers between devices: none -> 2.99 us  [body(): lax.ppermute(local_mass, 'dp', [(i, (i + k) % n_dp) for i in range(n_dp)])]
    ppermute x9, waiting for transfers between devices: 9.24 us -> 6.6 us  [swap(): return lax.ppermute(x, 'c', [(0, 1), (1, 0)])]
  transfers between devices with their start and end apart: 13 -> 15, of which waited for: 9 -> 9; matrix products, arithmetic and copies ran while one was open for 3% -> 4% of each run, Pallas kernels for 0% -> 0%
where the time goes in v1:
time: 205 us; the launch traced here: 201 us
  waiting for transfers between devices  75.8 us (37%)
  blocking collectives  73.6 us (36%)
  starting transfers between devices  21.4 us (10%)
  matrix products  19.2 us (9%)
  other arithmetic  5.27 us (3%)
  between operations  3.98 us (2%)
    all_to_all x2, blocking collectives, exchange(): return lax.all_to_all(x, axes, 0, 0)  73.6 us
    all_to_all x3, waiting for transfers between devices, exchange(): return lax.all_to_all(x, axes, 0, 0)  66.3 us
    all_to_all x3, starting transfers between devices, exchange(): return lax.all_to_all(x, axes, 0, 0)  16 us
    dot_general x6, matrix products, mm(): return jnp.dot(a, b, preferred_element_type=F32)  10.1 us
    dot_general x2, matrix products, mm_t(): lax.dot_general(a, b, (((1,), (1,)), ((), ())), preferred_element_type=F32)  6.94 us
    ppermute x9, waiting for transfers between devices, swap(): return lax.ppermute(x, 'c', [(0, 1), (1, 0)])  6.6 us
    ppermute x3, starting transfers between devices, body(): lax.ppermute(local_mass, 'dp', [(i, (i + k) % n_dp) for i in range(n_dp)])  4.15 us
  transfers between devices with their start and end apart: 15, of which 9 were waited for; matrix products, arithmetic and copies ran while one was open for 4% of the time, Pallas kernels for 0%

profile of v1, /device:TPU:2, one launch (start us, length us, event | category | flops | bytes accessed | tf_op | source)
XLA Modules:
  0.0 201.2 jit_solution(6696481786023745933)
XLA Ops:
  0.7 1.1 fusion.34
  1.7 0.9 fusion.36
  2.7 1.2 collective-permute-done.1
  4.0 39.8 %all_to_all.25 = bf16[32,8,2048]{2,1,0:T(8,128)(2,1)S(1)} all-to-all(bf16[32,8,2048]{2,1,0:T(8,128)(2,1)S(1)} %broadcast_in_dim.32), channel_id=1, replica_groups=mesh['dp'=4,'z'=8,'y'=4,'c'=2] {'z','y'}, dimensions={0} | all-to-all | bytes 2097152 | tf_op jit(solution)/shard_map/all_to_all | solution.py:61
  44.3 0.4 fusion.24
  44.7 1.7 collective-permute-done.2
  47.7 2.5 %collective-permute-done.3 = bf16[256,2048]{1,0:T(8,128)(2,1)S(1)} collective-permute-done((bf16[256,2048]{1,0:T(8,128)(2,1)S(1)}, bf16[256,2048]{1,0:T(8,128)(2,1)S(1)}, u32[]{:S(2)}, u32[]{:S(2)}) %collective-permute-start.3) | collective-permute-done | bytes 1048608 | tf_op jit(solution)/shard_map/ppermute | solution.py:30
  50.2 1.4 fusion.21
  51.6 5.7 %all-to-all-start.1 = ((bf16[32,8,2048]{2,1,0:T(8,128)(2,1)}), bf16[32,8,2048]{2,1,0:T(8,128)(2,1)S(1)}, u32[]{:S(2)}, u32[]{:S(2)}) async-start(bf16[32,8,2048]{2,1,0:T(8,128)(2,1)} %fusion.21), calls=%async_computation.1 | async-start | bytes 2097152 | tf_op jit(solution)/shard_map/all_to_all | solution.py:61
  57.5 28.2 %all-to-all-done.1 = bf16[32,8,2048]{2,1,0:T(8,128)(2,1)S(1)} async-done(((bf16[32,8,2048]{2,1,0:T(8,128)(2,1)}), bf16[32,8,2048]{2,1,0:T(8,128)(2,1)S(1)}, u32[]{:S(2)}, u32[]{:S(2)}) %all-to-all-start.1) | async-done | bytes 1048608 | tf_op jit(solution)/shard_map/all_to_all | solution.py:61
  86.1 1.1 collective-permute-done.4
  87.5 33.8 %all_to_all.26 = bf16[32,8,2048]{2,1,0:T(8,128)(2,1)S(1)} all-to-all(bf16[32,8,2048]{2,1,0:T(8,128)(2,1)S(1)} %broadcast_in_dim.59), channel_id=1, replica_groups=mesh['dp'=4,'z'=8,'y'=4,'c'=2] {'z','y'}, dimensions={0} | all-to-all | bytes 2097152 | tf_op jit(solution)/shard_map/all_to_all | solution.py:61
  121.4 3.5 %fusion.6 = f32[256,1024]{1,0:T(8,128)S(1)} fusion(bf16[4096,1024]{1,0:T(8,128)(2,1)} %param.15, s32[]{:T(128)} %select_n.65, bf16[32,8,2048]{2,1,0:T(8,128)(2,1)S(1)} %all_to_all.26), kind=kOutput, calls=%fused_computation.6 | convolution fusion | flops 1073741824 | bytes 6291968 | tf_op jit(solution)/shard_map/dot_general | solution.py:34
  124.9 3.9 %fusion.20 = (f32[256,1024]{1,0:T(8,128)S(1)}, f32[256,1024]{1,0:T(8,128)S(1)}) fusion(f32[256]{0:T(256)S(1)} %compare_convert_fusion, f32[256,1024]{1,0:T(8,128)S(1)} %fusion.6, bf16[256,2048]{1,0:T(8,128)(2,1)S(1)} %collective-permute-done.5, bf16[4096,1024]{1,0:T(8,128)(2,1)} %param.15, s32[]{:T(128)S(6)} %select_n.66), kind=kOutput, calls=%fused_computation.23 | convolution fusion | flops 1075576832 | bytes 8389636 | tf_op jit(solution)/shard_map/dot_general | solution.py:34
  128.8 1.5 fusion.56
  130.3 1.5 collective-permute-start.7
  131.8 0.5 collective-permute-start.8
  132.3 2.1 %collective-permute-start.6 = (f32[8,128]{1,0:T(8,128)S(1)}, f32[8,128]{1,0:T(8,128)S(1)}, u32[]{:S(2)}, u32[]{:S(2)}) collective-permute-start(f32[8,128]{1,0:T(8,128)S(1)} %bitcast.39), channel_id=1, source_target_pairs={{0,128},{64,192},{128,0},{192,64},{1,129},{65,193},{129,1},{193,65... | collective-permute-start | bytes 12296 | tf_op jit(solution)/shard_map/ppermute | solution.py:125
  134.5 0.9 collective-permute-done.8
  135.4 2.0 %collective-permute-done.6 = f32[8,128]{1,0:T(8,128)S(1)} collective-permute-done((f32[8,128]{1,0:T(8,128)S(1)}, f32[8,128]{1,0:T(8,128)S(1)}, u32[]{:S(2)}, u32[]{:S(2)}) %collective-permute-start.6) | collective-permute-done | bytes 4128 | tf_op jit(solution)/shard_map/ppermute | solution.py:125
  137.5 0.7 broadcast_in_dim.60
  138.2 6.2 %all-to-all-start.3 = ((f32[64,2,128]{2,1,0:T(2,128)}), f32[64,2,128]{2,1,0:T(2,128)S(1)}, u32[]{:S(2)}, u32[]{:S(2)}) async-start(f32[64,2,128]{2,1,0:T(2,128)} %broadcast_in_dim.60), calls=%async_computation.3 | async-start | bytes 131072 | tf_op jit(solution)/shard_map/all_to_all | solution.py:61
  144.4 0.6 convolution_multiply_fusion
  145.0 9.4 %all-to-all-done.3 = f32[64,2,128]{2,1,0:T(2,128)S(1)} async-done(((f32[64,2,128]{2,1,0:T(2,128)}), f32[64,2,128]{2,1,0:T(2,128)S(1)}, u32[]{:S(2)}, u32[]{:S(2)}) %all-to-all-start.3) | async-done | bytes 65568 | tf_op jit(solution)/shard_map/all_to_all | solution.py:61
  154.6 0.6 fusion.57
  155.9 3.5 %fusion.8 = bf16[256,2048]{1,0:T(8,128)(2,1)S(1)} fusion(bf16[256,1024]{1,0:T(8,128)(2,1)S(1)} %multiply_convert_fusion, bf16[4096,1024]{1,0:T(8,128)(2,1)} %param.15, s32[]{:T(128)S(6)} %select_n.66), kind=kOutput, calls=%fused_computation.8 | convolution fusion | flops 1074266112 | bytes 5767172 | tf_op jit(solution)/shard_map/dot_general | solution.py:38
  159.6 3.5 %fusion.4 = f32[256,2048]{1,0:T(8,128)S(1)} fusion(bf16[256,1024]{1,0:T(8,128)(2,1)S(1)} %multiply_convert_fusion, bf16[4096,1024]{1,0:T(8,128)(2,1)} %param.15, s32[]{:T(128)} %select_n.65), kind=kOutput, calls=%fused_computation.4 | convolution fusion | flops 1073741824 | bytes 6816256 | tf_op jit(solution)/shard_map/dot_general | solution.py:38
  163.1 1.3 fusion.22
  164.3 4.1 %all-to-all-start.4 = ((bf16[32,8,2048]{2,1,0:T(8,128)(2,1)}), bf16[32,8,2048]{2,1,0:T(8,128)(2,1)S(1)}, u32[]{:S(2)}, u32[]{:S(2)}) async-start(bf16[32,8,2048]{2,1,0:T(8,128)(2,1)} %fusion.22), calls=%async_computation.4 | async-start | bytes 2097152 | tf_op jit(solution)/shard_map/all_to_all | solution.py:61
  168.4 0.5 collective-permute-start.9
  168.9 28.7 %all-to-all-done.4 = bf16[32,8,2048]{2,1,0:T(8,128)(2,1)S(1)} async-done(((bf16[32,8,2048]{2,1,0:T(8,128)(2,1)}), bf16[32,8,2048]{2,1,0:T(8,128)(2,1)S(1)}, u32[]{:S(2)}, u32[]{:S(2)}) %all-to-all-start.4) | async-done | bytes 1048608 | tf_op jit(solution)/shard_map/all_to_all | solution.py:61
  199.4 0.7 multiply_subtract_fusion
  (58 shorter events, 3.8 us)
Async XLA Ops:
  0.6 46.4 %copy-start = (bf16[128,4096]{1,0:T(8,128)(2,1)S(1)}, bf16[128,4096]{1,0:T(8,128)(2,1)}, u32[]{:S(2)}) copy-start(bf16[128,4096]{1,0:T(8,128)(2,1)} %param.13) | copy-start | bytes 3145732
  0.6 43.2 %copy-start.1 = (bf16[4096,128]{1,0:T(8,128)(2,1)S(1)}, bf16[4096,128]{1,0:T(8,128)(2,1)}, u32[]{:S(2)}) copy-start(bf16[4096,128]{1,0:T(8,128)(2,1)} %param.11) | copy-start | bytes 3145732
  2.6 1.3 collective-permute-start.1
  4.0 40.0 %copy-start.2 = (bf16[4096,128]{1,0:T(8,128)(2,1)S(1)}, bf16[4096,128]{1,0:T(8,128)(2,1)}, u32[]{:S(2)}) copy-start(bf16[4096,128]{1,0:T(8,128)(2,1)} %param.12) | copy-start | bytes 3145732
  43.8 2.7 %collective-permute-start.2 = (bf16[256,2048]{1,0:T(8,128)(2,1)S(1)}, bf16[256,2048]{1,0:T(8,128)(2,1)S(1)}, u32[]{:S(2)}, u32[]{:S(2)}) collective-permute-start(bf16[256,2048]{1,0:T(8,128)(2,1)S(1)} %bitcast.31), channel_id=1, source_target_pairs={{0,1},{1,0},{2,3},{3,2},{4,5},{5,4},{6,7},{7,6},{8,9},{9,8},{10,11... | collective-permute-start | bytes 3145736 | tf_op jit(solution)/shard_map/ppermute | solution.py:30
  47.4 9.9 %copy-start.3 = (bf16[4,4096]{1,0:T(4,128)(2,1)S(1)}, bf16[4,4096]{1,0:T(4,128)(2,1)}, u32[]{:S(2)}) copy-start(bf16[4,4096]{1,0:T(4,128)(2,1)} %param.9) | copy-start | bytes 98308
  47.5 2.7 %collective-permute-start.3 = (bf16[256,2048]{1,0:T(8,128)(2,1)S(1)}, bf16[256,2048]{1,0:T(8,128)(2,1)S(1)}, u32[]{:S(2)}, u32[]{:S(2)}) collective-permute-start(bf16[256,2048]{1,0:T(8,128)(2,1)S(1)} %convolution_convert_fusion), channel_id=1, source_target_pairs={{0,1},{1,0},{2,3},{3,2},{4,5},{5,4},{6,7},{7,6},{8,9},{9,8},{10,11... | collective-permute-start | bytes 3145736 | tf_op jit(solution)/shard_map/ppermute | solution.py:30
  51.6 35.6 %dynamic-slice-start = ((f32[4096]{0:T(1024)}, s32[]{:T(128)}), f32[2048]{0:T(1024)S(1)}, s32[]{:S(2)}) async-start(f32[4096]{0:T(1024)} %param.14, s32[]{:T(128)} %select_n.65), calls=%async_computation.5 | async-start | bytes 16896 | tf_op jit(solution)/shard_map/dynamic-slice
  51.6 34.1 %all-to-all-start.1 = ((bf16[32,8,2048]{2,1,0:T(8,128)(2,1)}), bf16[32,8,2048]{2,1,0:T(8,128)(2,1)S(1)}, u32[]{:S(2)}, u32[]{:S(2)}) async-start(bf16[32,8,2048]{2,1,0:T(8,128)(2,1)} %fusion.21), calls=%async_computation.1 | async-start | bytes 2097152 | tf_op jit(solution)/shard_map/all_to_all | solution.py:61
  57.4 28.5 %collective-permute-start = (bf16[4,2048]{1,0:T(4,128)(2,1)S(1)}, bf16[4,2048]{1,0:T(4,128)(2,1)S(1)}, u32[]{:S(2)}, u32[]{:S(2)}) collective-permute-start(bf16[4,2048]{1,0:T(4,128)(2,1)S(1)} %get-tuple-element.18), channel_id=1, source_target_pairs={{0,1},{1,0},{2,3},{3,2},{4,5},{5,4},{6,7},{7,6},{8,9},{9,8},{10,11... | collective-permute-start | bytes 49160 | tf_op jit(solution)/shard_map/ppermute | solution.py:30
  57.5 63.7 %copy-start.5 = (s32[1,256]{1,0:T(1,128)S(1)}, s32[1,256]{1,0:T(1,128)}, u32[]{:S(2)}) copy-start(s32[1,256]{1,0:T(1,128)} %param.16) | copy-start | bytes 3076
  57.5 63.8 %copy-start.6 = (s32[1,4]{1,0:T(1,128)S(1)}, s32[1,4]{1,0:T(1,128)}, u32[]{:S(2)}) copy-start(s32[1,4]{1,0:T(1,128)} %param.17) | copy-start | bytes 52
  86.0 1.2 collective-permute-start.4
  121.2 3.7 %collective-permute-start.5 = (bf16[256,2048]{1,0:T(8,128)(2,1)S(1)}, bf16[256,2048]{1,0:T(8,128)(2,1)S(1)}, u32[]{:S(2)}, u32[]{:S(2)}) collective-permute-start(bf16[256,2048]{1,0:T(8,128)(2,1)S(1)} %bitcast.32), channel_id=1, source_target_pairs={{0,1},{1,0},{2,3},{3,2},{4,5},{5,4},{6,7},{7,6},{8,9},{9,8},{10,11... | collective-permute-start | bytes 3145736 | tf_op jit(solution)/shard_map/ppermute | solution.py:30
  130.3 4.2 %collective-permute-start.7 = (f32[8,128]{1,0:T(8,128)S(1)}, f32[8,128]{1,0:T(8,128)S(1)}, u32[]{:S(2)}, u32[]{:S(2)}) collective-permute-start(f32[8,128]{1,0:T(8,128)S(1)} %bitcast.37), channel_id=1, source_target_pairs={{0,64},{64,128},{128,192},{192,0},{1,65},{65,129},{129,193},{193,1... | collective-permute-start | bytes 12296 | tf_op jit(solution)/shard_map/ppermute | solution.py:125
  131.8 3.6 %collective-permute-start.8 = (f32[8,128]{1,0:T(8,128)S(1)}, f32[8,128]{1,0:T(8,128)S(1)}, u32[]{:S(2)}, u32[]{:S(2)}) collective-permute-start(f32[8,128]{1,0:T(8,128)S(1)} %bitcast.38), channel_id=1, source_target_pairs={{0,192},{64,0},{128,64},{192,128},{1,193},{65,1},{129,65},{193,129... | collective-permute-start | bytes 12296 | tf_op jit(solution)/shard_map/ppermute | solution.py:125
  132.3 5.1 %collective-permute-start.6 = (f32[8,128]{1,0:T(8,128)S(1)}, f32[8,128]{1,0:T(8,128)S(1)}, u32[]{:S(2)}, u32[]{:S(2)}) collective-permute-start(f32[8,128]{1,0:T(8,128)S(1)} %bitcast.39), channel_id=1, source_target_pairs={{0,128},{64,192},{128,0},{192,64},{1,129},{65,193},{129,1},{193,65... | collective-permute-start | bytes 12296 | tf_op jit(solution)/shard_map/ppermute | solution.py:125
  138.2 16.2 %all-to-all-start.3 = ((f32[64,2,128]{2,1,0:T(2,128)}), f32[64,2,128]{2,1,0:T(2,128)S(1)}, u32[]{:S(2)}, u32[]{:S(2)}) async-start(f32[64,2,128]{2,1,0:T(2,128)} %broadcast_in_dim.60), calls=%async_computation.3 | async-start | bytes 131072 | tf_op jit(solution)/shard_map/all_to_all | solution.py:61
  159.4 3.7 %collective-permute-start.10 = (bf16[256,2048]{1,0:T(8,128)(2,1)S(1)}, bf16[256,2048]{1,0:T(8,128)(2,1)S(1)}, u32[]{:S(2)}, u32[]{:S(2)}) collective-permute-start(bf16[256,2048]{1,0:T(8,128)(2,1)S(1)} %fusion.8), channel_id=1, source_target_pairs={{0,1},{1,0},{2,3},{3,2},{4,5},{5,4},{6,7},{7,6},{8,9},{9,8},{10,11... | collective-permute-start | bytes 3145736 | tf_op jit(solution)/shard_map/ppermute | solution.py:30
  164.3 34.8 %copy-start.4 = (f32[4096]{0:T(1024)S(1)}, f32[4096]{0:T(1024)}, u32[]{:S(2)}) copy-start(f32[4096]{0:T(1024)} %param.14) | copy-start | bytes 49156
  164.3 33.3 %all-to-all-start.4 = ((bf16[32,8,2048]{2,1,0:T(8,128)(2,1)}), bf16[32,8,2048]{2,1,0:T(8,128)(2,1)S(1)}, u32[]{:S(2)}, u32[]{:S(2)}) async-start(bf16[32,8,2048]{2,1,0:T(8,128)(2,1)} %fusion.22), calls=%async_computation.4 | async-start | bytes 2097152 | tf_op jit(solution)/shard_map/all_to_all | solution.py:61
  168.4 30.7 %collective-permute-start.9 = (f32[4,2048]{1,0:T(4,128)S(1)}, f32[4,2048]{1,0:T(4,128)S(1)}, u32[]{:S(2)}, u32[]{:S(2)}) collective-permute-start(f32[4,2048]{1,0:T(4,128)S(1)} %get-tuple-element.16), channel_id=1, source_target_pairs={{0,1},{1,0},{2,3},{3,2},{4,5},{5,4},{6,7},{7,6},{8,9},{9,8},{10,11... | collective-permute-start | bytes 98312 | tf_op jit(solution)/shard_map/ppermute | solution.py:30
  197.8 1.4 collective-permute-start.11

commit v2 on v1

--- a/solution.py
+++ b/solution.py
@@ -4,7 +4,6 @@
 from jax.sharding import Mesh, PartitionSpec as P
 
 
-PLANE = ("z", "y")
 ALL = ("dp", "z", "y", "c")
 MP = ("z", "y", "c")
 BF = jnp.bfloat16
@@ -61,16 +60,41 @@
     return lax.all_to_all(x, axes, 0, 0)
 
 
-def gather(block, n):
-    spread = jnp.broadcast_to(block[None], (n, *block.shape))
-    mine = exchange(spread, PLANE).reshape(-1, block.shape[-1])
+def along_y(x, k):
+    n = lax.axis_size("y")
+    return lax.ppermute(x, "y", [(i, (i + k) % n) for i in range(n)])
+
+
+def local_rows(x):
+    nz, ny = lax.axis_size("z"), lax.axis_size("y")
+    x = x.reshape(nz, ny, -1, *x.shape[1:])
+    x = lax.dynamic_slice_in_dim(jnp.concatenate([x, x], axis=1), lax.axis_index("y"), ny, 1)
+    return x.swapaxes(0, 1).reshape(-1, *x.shape[3:])
+
+
+def gather(block):
+    spread = jnp.broadcast_to(block[None], (lax.axis_size("z"), *block.shape))
+    plane = exchange(spread, "z").reshape(-1, block.shape[-1])
+    got = [along_y(plane, -k) for k in range(1, lax.axis_size("y"))]
+    mine = jnp.concatenate([plane, *got], axis=0)
     return mine, swap(mine)
 
 
-def scatter(own, other, n):
+def both_halves(mine, theirs, weight, core):
+    own, other = halves(weight, core, 0)
+    first = lax.optimization_barrier(mm(mine, own))
+    return first + mm(theirs, other)
+
+
+def scatter(own, other):
     got = swap(other)
-    both = (own + got.astype(F32)).astype(BF)
-    moved = exchange(both.reshape(n, -1, both.shape[-1]), PLANE)
+    ny, nz = lax.axis_size("y"), lax.axis_size("z")
+    own, got = jnp.split(own, ny), jnp.split(got, ny)
+    both = [a + b.astype(F32) for a, b in zip(own, got)]
+    for k in range(1, ny):
+        both[k] = along_y(both[k].astype(BF), k).astype(F32)
+    plane = sum(both).astype(BF)
+    moved = exchange(plane.reshape(nz, -1, plane.shape[-1]), "z")
     return jnp.sum(moved.astype(F32), axis=0)
 
 
@@ -87,34 +111,32 @@
 ):
     highest = lax.Precision.HIGHEST
     core = lax.axis_index("c")
-    n = lax.axis_size(PLANE)
     n_dp = lax.axis_size("dp")
     n_mp = lax.axis_size(MP)
     own_rows = residual.astype(F32)
     normed_in = (own_rows * rms_scale(own_rows) * ffn_gain).astype(BF)
     member, valid = pool_masks(passage_ids[0], valid_counts[0])
+    member, valid = local_rows(member), local_rows(valid)
     gate_up = jnp.concatenate([gate_weight, up_weight], axis=1)
-    mine, theirs = gather(chip_rows(normed_in, core), n)
+    mine, theirs = gather(chip_rows(normed_in, core))
     residual8 = chip_rows(residual, core).astype(F32)
     gain8 = halves(final_gain[None, :], core, 1)[0]
 
-    gu_own, gu_other = halves(gate_up, core, 0)
-    gu = mm(mine, gu_own) + mm(theirs, gu_other)
+    gu = both_halves(mine, theirs, gate_up, core)
     hid = gate_weight.shape[1]
     activated = (jax.nn.silu(gu[:, :hid]) * gu[:, hid:]).astype(BF)
     down_own, down_other = halves(down_weight, core, 1)
     other = mm(activated, down_other).astype(BF)
-    hidden8 = residual8 + scatter(mm(activated, down_own), other, n)
+    hidden8 = residual8 + scatter(mm(activated, down_own), other)
     square = jnp.sum(hidden8 * hidden8, axis=1, keepdims=True)
     width = residual.shape[1]
     scale8 = lax.rsqrt((square + swap(square)) / width + 1e-05)
     normed8 = (hidden8 * scale8 * gain8).astype(BF)
-    mine, theirs = gather(normed8, n)
+    mine, theirs = gather(normed8)
     hidden = core_rows(hidden8, core)
     scale = rms_scale(hidden)
 
-    head_own, head_other = halves(head_weight, core, 0)
-    logits = mm(mine, head_own) + mm(theirs, head_other)
+    logits = both_halves(mine, theirs, head_weight, core)
     positive = jnp.maximum(logits, 0.0)
     weights = jnp.log1p(positive)
     powered = valid[:, None] * weights**4
@@ -137,9 +159,10 @@
     entropy = jnp.log(total) - spread / total
     slope_mass = jnp.log(total) - log_smooth.reshape(-1)
     slope_logit = lax.optimization_barrier((slope * slope_mass[None, :]).astype(BF))
+    head_own, head_other = halves(head_weight, core, 0)
     other = mm_t(slope_logit, head_other).astype(BF)
     own = lax.optimization_barrier(mm_t(slope_logit, head_own))
-    slope_normed = core_rows(scatter(own, other, n), core)
+    slope_normed = core_rows(scatter(own, other), core)
     scaled_slope = slope_normed * final_gain
     grad_hidden = scale * scaled_slope - hidden * scale**3 * jnp.mean(
         scaled_slope * hidden, axis=-1, keepdims=True

time: 205 us -> 194 us (0.946)
  blocking collectives: 73.6 us -> 35.4 us
  waiting for transfers between devices: 75.8 us -> 89.6 us
  starting transfers between devices: 21.4 us -> 33.5 us
    ppermute x0 -> x12, waiting for transfers between devices: none -> 46.9 us  [along_y(): return lax.ppermute(x, 'y', [(i, (i + k) % n) for i in range(n)])]
    all_to_all x2, blocking collectives: 73.6 us -> 35.4 us  [exchange(): return lax.all_to_all(x, axes, 0, 0)]
    all_to_all x3, waiting for transfers between devices: 66.3 us -> 33.6 us  [exchange(): return lax.all_to_all(x, axes, 0, 0)]
    ppermute x0 -> x12, starting transfers between devices: none -> 16.4 us  [along_y(): return lax.ppermute(x, 'y', [(i, (i + k) % n) for i in range(n)])]
    all_to_all x3, starting transfers between devices: 16 us -> 11.8 us  [exchange(): return lax.all_to_all(x, axes, 0, 0)]
  transfers between devices with their start and end apart: 15 -> 27, of which waited for: 9 -> 18; matrix products, arithmetic and copies ran while one was open for 4% -> 6% of each run, Pallas kernels for 0% -> 0%
where the time goes in v2:
time: 194 us; the launch traced here: 191 us
  waiting for transfers between devices  89.6 us (46%)
  blocking collectives  35.4 us (18%)
  starting transfers between devices  33.5 us (17%)
  matrix products  18.5 us (10%)
  other arithmetic  6.87 us (4%)
  between operations  4.3 us (2%)
  local copies, waits for them, and re-layouts  2.83 us (1%)
    ppermute x12, waiting for transfers between devices, along_y(): return lax.ppermute(x, 'y', [(i, (i + k) % n) for i in range(n)])  46.9 us
    all_to_all x2, blocking collectives, exchange(): return lax.all_to_all(x, axes, 0, 0)  35.4 us
    all_to_all x3, waiting for transfers between devices, exchange(): return lax.all_to_all(x, axes, 0, 0)  33.6 us
    ppermute x12, starting transfers between devices, along_y(): return lax.ppermute(x, 'y', [(i, (i + k) % n) for i in range(n)])  16.4 us
    all_to_all x3, starting transfers between devices, exchange(): return lax.all_to_all(x, axes, 0, 0)  11.8 us
    dot_general x6, matrix products, mm(): return jnp.dot(a, b, preferred_element_type=F32)  9.42 us
    dot_general x2, matrix products, mm_t(): lax.dot_general(a, b, (((1,), (1,)), ((), ())), preferred_element_type=F32)  6.94 us
    ppermute x9, waiting for transfers between devices, swap(): return lax.ppermute(x, 'c', [(0, 1), (1, 0)])  6.13 us
  transfers between devices with their start and end apart: 27, of which 18 were waited for; matrix products, arithmetic and copies ran while one was open for 6% of the time, Pallas kernels for 0%

profile of v2, /device:TPU:2, one launch (start us, length us, event | category | flops | bytes accessed | tf_op | source)
XLA Modules:
  0.0 190.9 jit_solution(14869910072092888033)
XLA Ops:
  3.9 20.5 %all_to_all.25 = bf16[8,8,2048]{2,1,0:T(8,128)(2,1)S(1)} all-to-all(bf16[8,8,2048]{2,1,0:T(8,128)(2,1)S(1)} %broadcast_in_dim.55), channel_id=1, replica_groups=mesh['dp'=4,'z'=8,'y'=4,'c'=2] {'z'}, dimensions={0} | all-to-all | bytes 524288 | tf_op jit(solution)/shard_map/all_to_all | solution.py:60
  24.4 1.6 collective-permute-start.4
  26.0 2.9 %collective-permute-start.3 = (bf16[64,2048]{1,0:T(8,128)(2,1)S(1)}, bf16[64,2048]{1,0:T(8,128)(2,1)S(1)}, u32[]{:S(2)}, u32[]{:S(2)}) collective-permute-start(bf16[64,2048]{1,0:T(8,128)(2,1)S(1)} %bitcast.43), channel_id=1, source_target_pairs={{0,4},{2,6},{4,0},{6,2},{1,5},{3,7},{5,1},{7,3},{8,12},{10,14},{12... | collective-permute-start | bytes 786440 | tf_op jit(solution)/shard_map/ppermute | solution.py:65
  28.9 1.3 collective-permute-start.2
  30.2 3.4 %collective-permute-done.4 = bf16[64,2048]{1,0:T(8,128)(2,1)S(1)} collective-permute-done((bf16[64,2048]{1,0:T(8,128)(2,1)S(1)}, bf16[64,2048]{1,0:T(8,128)(2,1)S(1)}, u32[]{:S(2)}, u32[]{:S(2)}) %collective-permute-start.4) | collective-permute-done | bytes 262176 | tf_op jit(solution)/shard_map/ppermute | solution.py:65
  33.7 5.9 %collective-permute-done.3 = bf16[64,2048]{1,0:T(8,128)(2,1)S(1)} collective-permute-done((bf16[64,2048]{1,0:T(8,128)(2,1)S(1)}, bf16[64,2048]{1,0:T(8,128)(2,1)S(1)}, u32[]{:S(2)}, u32[]{:S(2)}) %collective-permute-start.3) | collective-permute-done | bytes 262176 | tf_op jit(solution)/shard_map/ppermute | solution.py:65
  40.8 1.7 collective-permute-done.5
  44.1 2.1 %collective-permute-done.6 = bf16[256,2048]{1,0:T(8,128)(2,1)S(1)} collective-permute-done((bf16[256,2048]{1,0:T(8,128)(2,1)S(1)}, bf16[256,2048]{1,0:T(8,128)(2,1)S(1)}, u32[]{:S(2)}, u32[]{:S(2)}) %collective-permute-start.6) | collective-permute-done | bytes 1048608 | tf_op jit(solution)/shard_map/ppermute | solution.py:29
  46.4 2.1 %collective-permute-start.9 = (bf16[64,2048]{1,0:T(8,128)(2,1)S(1)}, bf16[64,2048]{1,0:T(8,128)(2,1)S(1)}, u32[]{:S(2)}, u32[]{:S(2)}) collective-permute-start(bf16[64,2048]{1,0:T(8,128)(2,1)S(1)} %get-tuple-element.18), channel_id=1, source_target_pairs={{0,6},{2,0},{4,2},{6,4},{1,7},{3,1},{5,3},{7,5},{8,14},{10,8},{12,... | collective-permute-start | bytes 786440 | tf_op jit(solution)/shard_map/ppermute | solution.py:65
  50.5 9.6 %collective-permute-done.9 = bf16[64,2048]{1,0:T(8,128)(2,1)S(1)} collective-permute-done((bf16[64,2048]{1,0:T(8,128)(2,1)S(1)}, bf16[64,2048]{1,0:T(8,128)(2,1)S(1)}, u32[]{:S(2)}, u32[]{:S(2)}) %collective-permute-start.9) | collective-permute-done | bytes 262176 | tf_op jit(solution)/shard_map/ppermute | solution.py:65
  60.1 3.7 %collective-permute-done.7 = bf16[64,2048]{1,0:T(8,128)(2,1)S(1)} collective-permute-done((bf16[64,2048]{1,0:T(8,128)(2,1)S(1)}, bf16[64,2048]{1,0:T(8,128)(2,1)S(1)}, u32[]{:S(2)}, u32[]{:S(2)}) %collective-permute-start.7) | collective-permute-done | bytes 262176 | tf_op jit(solution)/shard_map/ppermute | solution.py:65
  64.6 3.5 %all-to-all-start.1 = ((bf16[8,8,2048]{2,1,0:T(8,128)(2,1)}), bf16[8,8,2048]{2,1,0:T(8,128)(2,1)S(1)}, u32[]{:S(2)}, u32[]{:S(2)}) async-start(bf16[8,8,2048]{2,1,0:T(8,128)(2,1)} %fusion.38), calls=%async_computation.1 | async-start | bytes 524288 | tf_op jit(solution)/shard_map/all_to_all | solution.py:60
  68.3 12.1 %all-to-all-done.1 = bf16[8,8,2048]{2,1,0:T(8,128)(2,1)S(1)} async-done(((bf16[8,8,2048]{2,1,0:T(8,128)(2,1)}), bf16[8,8,2048]{2,1,0:T(8,128)(2,1)S(1)}, u32[]{:S(2)}, u32[]{:S(2)}) %all-to-all-start.1) | async-done | bytes 262176 | tf_op jit(solution)/shard_map/all_to_all | solution.py:60
  82.0 14.9 %all_to_all.26 = bf16[8,8,2048]{2,1,0:T(8,128)(2,1)S(1)} all-to-all(bf16[8,8,2048]{2,1,0:T(8,128)(2,1)S(1)} %broadcast_in_dim.57), channel_id=1, replica_groups=mesh['dp'=4,'z'=8,'y'=4,'c'=2] {'z'}, dimensions={0} | all-to-all | bytes 524288 | tf_op jit(solution)/shard_map/all_to_all | solution.py:60
  98.0 2.6 %collective-permute-start.11 = (bf16[64,2048]{1,0:T(8,128)(2,1)S(1)}, bf16[64,2048]{1,0:T(8,128)(2,1)S(1)}, u32[]{:S(2)}, u32[]{:S(2)}) collective-permute-start(bf16[64,2048]{1,0:T(8,128)(2,1)S(1)} %bitcast.39), channel_id=1, source_target_pairs={{0,6},{2,0},{4,2},{6,4},{1,7},{3,1},{5,3},{7,5},{8,14},{10,8},{12,... | collective-permute-start | bytes 786440 | tf_op jit(solution)/shard_map/ppermute | solution.py:65
  101.9 10.0 %collective-permute-done.13 = bf16[64,2048]{1,0:T(8,128)(2,1)S(1)} collective-permute-done((bf16[64,2048]{1,0:T(8,128)(2,1)S(1)}, bf16[64,2048]{1,0:T(8,128)(2,1)S(1)}, u32[]{:S(2)}, u32[]{:S(2)}) %collective-permute-start.13) | collective-permute-done | bytes 262176 | tf_op jit(solution)/shard_map/ppermute | solution.py:65
  113.5 3.4 %fusion.6 = f32[256,1024]{1,0:T(8,128)S(1)} fusion(bf16[4096,1024]{1,0:T(8,128)(2,1)} %param.15, s32[]{:T(128)} %select_n.72, bf16[64,2048]{1,0:T(8,128)(2,1)S(1)} %collective-permute-done.13, bf16[64,2048]{1,0:T(8,128)(2,1)S(1)} %collective-permute-done.12, bf16[64,2048]{1,0:T(8,128)(2,1)S(1)} %collective-permute-done.11, bf16[64,2048]{1,0:T(8,128)(2,1)S(1)} %bitcast.41), kind=kOutput, calls=%fused_computation.6 | convolution fusion | flops 1077936128 | bytes 6291968 | tf_op jit(solution)/shard_map/dot_general | solution.py:33
  117.0 4.2 %fusion.14 = (f32[256,1024]{1,0:T(8,128)S(1)}, f32[256,1024]{1,0:T(8,128)S(1)}) fusion(f32[256]{0:T(256)S(1)} %mul.154, f32[256,1024]{1,0:T(8,128)S(1)} %fusion.6, bf16[256,2048]{1,0:T(8,128)(2,1)} %collective-permute-done.14, bf16[4096,1024]{1,0:T(8,128)(2,1)} %param.15, s32[]{:T(128)S(6)} %select_n.73), kind=kOutput, calls=%fused_computation.16 | convolution fusion | flops 1075576832 | bytes 8389636 | tf_op jit(solution)/shard_map/dot_general | solution.py:33
  121.2 1.5 fusion.63
  122.8 1.5 collective-permute-start.16
  124.8 2.1 %collective-permute-start.15 = (f32[8,128]{1,0:T(8,128)S(1)}, f32[8,128]{1,0:T(8,128)S(1)}, u32[]{:S(2)}, u32[]{:S(2)}) collective-permute-start(f32[8,128]{1,0:T(8,128)S(1)} %bitcast.49), channel_id=1, source_target_pairs={{0,128},{64,192},{128,0},{192,64},{1,129},{65,193},{129,1},{193,65... | collective-permute-start | bytes 12296 | tf_op jit(solution)/shard_map/ppermute | solution.py:147
  127.9 2.0 %collective-permute-done.15 = f32[8,128]{1,0:T(8,128)S(1)} collective-permute-done((f32[8,128]{1,0:T(8,128)S(1)}, f32[8,128]{1,0:T(8,128)S(1)}, u32[]{:S(2)}, u32[]{:S(2)}) %collective-permute-start.15) | collective-permute-done | bytes 4128 | tf_op jit(solution)/shard_map/ppermute | solution.py:147
  130.6 4.9 %all-to-all-start.3 = ((f32[64,2,128]{2,1,0:T(2,128)}), f32[64,2,128]{2,1,0:T(2,128)S(1)}, u32[]{:S(2)}, u32[]{:S(2)}) async-start(f32[64,2,128]{2,1,0:T(2,128)} %broadcast_in_dim.58), calls=%async_computation.3 | async-start | bytes 131072 | tf_op jit(solution)/shard_map/all_to_all | solution.py:60
  136.2 9.4 %all-to-all-done.3 = f32[64,2,128]{2,1,0:T(2,128)S(1)} async-done(((f32[64,2,128]{2,1,0:T(2,128)}), f32[64,2,128]{2,1,0:T(2,128)S(1)}, u32[]{:S(2)}, u32[]{:S(2)}) %all-to-all-start.3) | async-done | bytes 65568 | tf_op jit(solution)/shard_map/all_to_all | solution.py:60
  147.1 3.5 %fusion.8 = bf16[256,2048]{1,0:T(8,128)(2,1)S(1)} fusion(bf16[256,1024]{1,0:T(8,128)(2,1)S(1)} %multiply_convert_fusion, bf16[4096,1024]{1,0:T(8,128)(2,1)} %param.15, s32[]{:T(128)S(6)} %select_n.73), kind=kOutput, calls=%fused_computation.8 | convolution fusion | flops 1074266112 | bytes 5767172 | tf_op jit(solution)/shard_map/dot_general | solution.py:37
  150.8 3.5 %fusion.4 = f32[256,2048]{1,0:T(8,128)S(1)} fusion(bf16[256,1024]{1,0:T(8,128)(2,1)S(1)} %multiply_convert_fusion, bf16[4096,1024]{1,0:T(8,128)(2,1)} %param.15, s32[]{:T(128)} %select_n.72), kind=kOutput, calls=%fused_computation.4 | convolution fusion | flops 1073741824 | bytes 6816256 | tf_op jit(solution)/shard_map/dot_general | solution.py:37
  155.4 1.7 collective-permute-start.21
  157.2 6.5 %collective-permute-done.22 = bf16[64,2048]{1,0:T(8,128)(2,1)S(1)} collective-permute-done((bf16[64,2048]{1,0:T(8,128)(2,1)S(1)}, bf16[64,2048]{1,0:T(8,128)(2,1)S(1)}, u32[]{:S(2)}, u32[]{:S(2)}) %collective-permute-start.22) | collective-permute-done | bytes 262176 | tf_op jit(solution)/shard_map/ppermute | solution.py:65
  163.7 2.3 %collective-permute-done.21 = bf16[64,2048]{1,0:T(8,128)(2,1)S(1)} collective-permute-done((bf16[64,2048]{1,0:T(8,128)(2,1)S(1)}, bf16[64,2048]{1,0:T(8,128)(2,1)S(1)}, u32[]{:S(2)}, u32[]{:S(2)}) %collective-permute-start.21) | collective-permute-done | bytes 262176 | tf_op jit(solution)/shard_map/ppermute | solution.py:65
  166.1 4.7 %collective-permute-done.20 = bf16[64,2048]{1,0:T(8,128)(2,1)S(1)} collective-permute-done((bf16[64,2048]{1,0:T(8,128)(2,1)S(1)}, bf16[64,2048]{1,0:T(8,128)(2,1)S(1)}, u32[]{:S(2)}, u32[]{:S(2)}) %collective-permute-start.20) | collective-permute-done | bytes 262176 | tf_op jit(solution)/shard_map/ppermute | solution.py:65
  171.7 3.4 %all-to-all-start.4 = ((bf16[8,8,2048]{2,1,0:T(8,128)(2,1)}), bf16[8,8,2048]{2,1,0:T(8,128)(2,1)S(1)}, u32[]{:S(2)}, u32[]{:S(2)}) async-start(bf16[8,8,2048]{2,1,0:T(8,128)(2,1)} %fusion.39), calls=%async_computation.4 | async-start | bytes 524288 | tf_op jit(solution)/shard_map/all_to_all | solution.py:60
  175.2 12.1 %all-to-all-done.4 = bf16[8,8,2048]{2,1,0:T(8,128)(2,1)S(1)} async-done(((bf16[8,8,2048]{2,1,0:T(8,128)(2,1)}), bf16[8,8,2048]{2,1,0:T(8,128)(2,1)S(1)}, u32[]{:S(2)}, u32[]{:S(2)}) %all-to-all-start.4) | async-done | bytes 262176 | tf_op jit(solution)/shard_map/all_to_all | solution.py:60
  (100 shorter events, 21.7 us)
Async XLA Ops:
  0.6 42.4 %copy-start = (bf16[128,4096]{1,0:T(8,128)(2,1)S(1)}, bf16[128,4096]{1,0:T(8,128)(2,1)}, u32[]{:S(2)}) copy-start(bf16[128,4096]{1,0:T(8,128)(2,1)} %param.13) | copy-start | bytes 3145732
  0.6 39.2 %copy-start.1 = (bf16[4096,128]{1,0:T(8,128)(2,1)S(1)}, bf16[4096,128]{1,0:T(8,128)(2,1)}, u32[]{:S(2)}) copy-start(bf16[4096,128]{1,0:T(8,128)(2,1)} %param.11) | copy-start | bytes 3145732
  2.6 1.3 collective-permute-start.1
  24.4 9.3 %collective-permute-start.4 = (bf16[64,2048]{1,0:T(8,128)(2,1)S(1)}, bf16[64,2048]{1,0:T(8,128)(2,1)S(1)}, u32[]{:S(2)}, u32[]{:S(2)}) collective-permute-start(bf16[64,2048]{1,0:T(8,128)(2,1)S(1)} %bitcast.42), channel_id=1, source_target_pairs={{0,2},{2,4},{4,6},{6,0},{1,3},{3,5},{5,7},{7,1},{8,10},{10,12},{12... | collective-permute-start | bytes 786440 | tf_op jit(solution)/shard_map/ppermute | solution.py:65
  26.0 13.6 %collective-permute-start.3 = (bf16[64,2048]{1,0:T(8,128)(2,1)S(1)}, bf16[64,2048]{1,0:T(8,128)(2,1)S(1)}, u32[]{:S(2)}, u32[]{:S(2)}) collective-permute-start(bf16[64,2048]{1,0:T(8,128)(2,1)S(1)} %bitcast.43), channel_id=1, source_target_pairs={{0,4},{2,6},{4,0},{6,2},{1,5},{3,7},{5,1},{7,3},{8,12},{10,14},{12... | collective-permute-start | bytes 786440 | tf_op jit(solution)/shard_map/ppermute | solution.py:65
  28.9 10.7 %collective-permute-start.2 = (bf16[64,2048]{1,0:T(8,128)(2,1)S(1)}, bf16[64,2048]{1,0:T(8,128)(2,1)S(1)}, u32[]{:S(2)}, u32[]{:S(2)}) collective-permute-start(bf16[64,2048]{1,0:T(8,128)(2,1)S(1)} %bitcast.44), channel_id=1, source_target_pairs={{0,6},{2,0},{4,2},{6,4},{1,7},{3,1},{5,3},{7,5},{8,14},{10,8},{12,... | collective-permute-start | bytes 786440 | tf_op jit(solution)/shard_map/ppermute | solution.py:65
  39.7 2.7 %collective-permute-start.5 = (bf16[256,2048]{1,0:T(8,128)(2,1)S(1)}, bf16[256,2048]{1,0:T(8,128)(2,1)S(1)}, u32[]{:S(2)}, u32[]{:S(2)}) collective-permute-start(bf16[256,2048]{1,0:T(8,128)(2,1)S(1)} %pad_maximum_fusion), channel_id=1, source_target_pairs={{0,1},{1,0},{2,3},{3,2},{4,5},{5,4},{6,7},{7,6},{8,9},{9,8},{10,11... | collective-permute-start | bytes 3145736 | tf_op jit(solution)/shard_map/ppermute | solution.py:29
  43.5 2.7 %collective-permute-start.6 = (bf16[256,2048]{1,0:T(8,128)(2,1)S(1)}, bf16[256,2048]{1,0:T(8,128)(2,1)S(1)}, u32[]{:S(2)}, u32[]{:S(2)}) collective-permute-start(bf16[256,2048]{1,0:T(8,128)(2,1)S(1)} %convolution_convert_fusion), channel_id=1, source_target_pairs={{0,1},{1,0},{2,3},{3,2},{4,5},{5,4},{6,7},{7,6},{8,9},{9,8},{10,11... | collective-permute-start | bytes 3145736 | tf_op jit(solution)/shard_map/ppermute | solution.py:29
  46.4 35.5 %dynamic-slice-start = ((f32[4096]{0:T(1024)}, s32[]{:T(128)}), f32[2048]{0:T(1024)S(1)}, s32[]{:S(2)}) async-start(f32[4096]{0:T(1024)} %param.14, s32[]{:T(128)} %select_n.72), calls=%async_computation.5 | async-start | bytes 16896 | tf_op jit(solution)/shard_map/dynamic-slice
  46.4 54.8 %copy-start.5 = (s32[1,256]{1,0:T(1,128)S(1)}, s32[1,256]{1,0:T(1,128)}, u32[]{:S(2)}) copy-start(s32[1,256]{1,0:T(1,128)} %param.16) | copy-start | bytes 3076
  46.4 13.7 %collective-permute-start.9 = (bf16[64,2048]{1,0:T(8,128)(2,1)S(1)}, bf16[64,2048]{1,0:T(8,128)(2,1)S(1)}, u32[]{:S(2)}, u32[]{:S(2)}) collective-permute-start(bf16[64,2048]{1,0:T(8,128)(2,1)S(1)} %get-tuple-element.18), channel_id=1, source_target_pairs={{0,6},{2,0},{4,2},{6,4},{1,7},{3,1},{5,3},{7,5},{8,14},{10,8},{12,... | collective-permute-start | bytes 786440 | tf_op jit(solution)/shard_map/ppermute | solution.py:65
  48.6 11.5 %collective-permute-start.8 = (bf16[64,2048]{1,0:T(8,128)(2,1)S(1)}, bf16[64,2048]{1,0:T(8,128)(2,1)S(1)}, u32[]{:S(2)}, u32[]{:S(2)}) collective-permute-start(bf16[64,2048]{1,0:T(8,128)(2,1)S(1)} %get-tuple-element.19), channel_id=1, source_target_pairs={{0,4},{2,6},{4,0},{6,2},{1,5},{3,7},{5,1},{7,3},{8,12},{10,14},{12... | collective-permute-start | bytes 786440 | tf_op jit(solution)/shard_map/ppermute | solution.py:65
  49.7 14.1 %collective-permute-start.7 = (bf16[64,2048]{1,0:T(8,128)(2,1)S(1)}, bf16[64,2048]{1,0:T(8,128)(2,1)S(1)}, u32[]{:S(2)}, u32[]{:S(2)}) collective-permute-start(bf16[64,2048]{1,0:T(8,128)(2,1)S(1)} %get-tuple-element.17), channel_id=1, source_target_pairs={{0,2},{2,4},{4,6},{6,0},{1,3},{3,5},{5,7},{7,1},{8,10},{10,12},{12... | collective-permute-start | bytes 786440 | tf_op jit(solution)/shard_map/ppermute | solution.py:65
  64.6 48.5 %copy-start.6 = (s32[1,4]{1,0:T(1,128)S(1)}, s32[1,4]{1,0:T(1,128)}, u32[]{:S(2)}) copy-start(s32[1,4]{1,0:T(1,128)} %param.17) | copy-start | bytes 52
  64.6 15.8 %all-to-all-start.1 = ((bf16[8,8,2048]{2,1,0:T(8,128)(2,1)}), bf16[8,8,2048]{2,1,0:T(8,128)(2,1)S(1)}, u32[]{:S(2)}, u32[]{:S(2)}) async-start(bf16[8,8,2048]{2,1,0:T(8,128)(2,1)} %fusion.38), calls=%async_computation.1 | async-start | bytes 524288 | tf_op jit(solution)/shard_map/all_to_all | solution.py:60
  68.2 12.3 %collective-permute-start = (bf16[4,2048]{1,0:T(4,128)(2,1)S(1)}, bf16[4,2048]{1,0:T(4,128)(2,1)S(1)}, u32[]{:S(2)}, u32[]{:S(2)}) collective-permute-start(bf16[4,2048]{1,0:T(4,128)(2,1)S(1)} %get-tuple-element.24), channel_id=1, source_target_pairs={{0,1},{1,0},{2,3},{3,2},{4,5},{5,4},{6,7},{7,6},{8,9},{9,8},{10,11... | collective-permute-start | bytes 49160 | tf_op jit(solution)/shard_map/ppermute | solution.py:29
  80.6 1.2 collective-permute-start.10
  96.9 15.1 %collective-permute-start.13 = (bf16[64,2048]{1,0:T(8,128)(2,1)S(1)}, bf16[64,2048]{1,0:T(8,128)(2,1)S(1)}, u32[]{:S(2)}, u32[]{:S(2)}) collective-permute-start(bf16[64,2048]{1,0:T(8,128)(2,1)S(1)} %bitcast.37), channel_id=1, source_target_pairs={{0,2},{2,4},{4,6},{6,0},{1,3},{3,5},{5,7},{7,1},{8,10},{10,12},{12... | collective-permute-start | bytes 786440 | tf_op jit(solution)/shard_map/ppermute | solution.py:65
  96.9 15.1 %collective-permute-start.12 = (bf16[64,2048]{1,0:T(8,128)(2,1)S(1)}, bf16[64,2048]{1,0:T(8,128)(2,1)S(1)}, u32[]{:S(2)}, u32[]{:S(2)}) collective-permute-start(bf16[64,2048]{1,0:T(8,128)(2,1)S(1)} %bitcast.38), channel_id=1, source_target_pairs={{0,4},{2,6},{4,0},{6,2},{1,5},{3,7},{5,1},{7,3},{8,12},{10,14},{12... | collective-permute-start | bytes 786440 | tf_op jit(solution)/shard_map/ppermute | solution.py:65
  98.0 14.6 %collective-permute-start.11 = (bf16[64,2048]{1,0:T(8,128)(2,1)S(1)}, bf16[64,2048]{1,0:T(8,128)(2,1)S(1)}, u32[]{:S(2)}, u32[]{:S(2)}) collective-permute-start(bf16[64,2048]{1,0:T(8,128)(2,1)S(1)} %bitcast.39), channel_id=1, source_target_pairs={{0,6},{2,0},{4,2},{6,4},{1,7},{3,1},{5,3},{7,5},{8,14},{10,8},{12,... | collective-permute-start | bytes 786440 | tf_op jit(solution)/shard_map/ppermute | solution.py:65
  112.7 4.3 %collective-permute-start.14 = (bf16[256,2048]{1,0:T(8,128)(2,1)S(1)}, bf16[256,2048]{1,0:T(8,128)(2,1)}, u32[]{:S(2)}, u32[]{:S(2)}) collective-permute-start(bf16[256,2048]{1,0:T(8,128)(2,1)S(1)} %pad_maximum_fusion.1), channel_id=1, source_target_pairs={{0,1},{1,0},{2,3},{3,2},{4,5},{5,4},{6,7},{7,6},{8,9},{9,8},{10,11... | collective-permute-start | bytes 3145736 | tf_op jit(solution)/shard_map/ppermute | solution.py:29
  122.8 4.2 %collective-permute-start.16 = (f32[8,128]{1,0:T(8,128)S(1)}, f32[8,128]{1,0:T(8,128)S(1)}, u32[]{:S(2)}, u32[]{:S(2)}) collective-permute-start(f32[8,128]{1,0:T(8,128)S(1)} %bitcast.47), channel_id=1, source_target_pairs={{0,64},{64,128},{128,192},{192,0},{1,65},{65,129},{129,193},{193,1... | collective-permute-start | bytes 12296 | tf_op jit(solution)/shard_map/ppermute | solution.py:147
  124.3 3.6 %collective-permute-start.17 = (f32[8,128]{1,0:T(8,128)S(1)}, f32[8,128]{1,0:T(8,128)S(1)}, u32[]{:S(2)}, u32[]{:S(2)}) collective-permute-start(f32[8,128]{1,0:T(8,128)S(1)} %bitcast.48), channel_id=1, source_target_pairs={{0,192},{64,0},{128,64},{192,128},{1,193},{65,1},{129,65},{193,129... | collective-permute-start | bytes 12296 | tf_op jit(solution)/shard_map/ppermute | solution.py:147
  124.8 5.1 %collective-permute-start.15 = (f32[8,128]{1,0:T(8,128)S(1)}, f32[8,128]{1,0:T(8,128)S(1)}, u32[]{:S(2)}, u32[]{:S(2)}) collective-permute-start(f32[8,128]{1,0:T(8,128)S(1)} %bitcast.49), channel_id=1, source_target_pairs={{0,128},{64,192},{128,0},{192,64},{1,129},{65,193},{129,1},{193,65... | collective-permute-start | bytes 12296 | tf_op jit(solution)/shard_map/ppermute | solution.py:147
  130.6 14.9 %all-to-all-start.3 = ((f32[64,2,128]{2,1,0:T(2,128)}), f32[64,2,128]{2,1,0:T(2,128)S(1)}, u32[]{:S(2)}, u32[]{:S(2)}) async-start(f32[64,2,128]{2,1,0:T(2,128)} %broadcast_in_dim.58), calls=%async_computation.3 | async-start | bytes 131072 | tf_op jit(solution)/shard_map/all_to_all | solution.py:60
  150.6 3.7 %collective-permute-start.19 = (bf16[256,2048]{1,0:T(8,128)(2,1)S(1)}, bf16[256,2048]{1,0:T(8,128)(2,1)S(1)}, u32[]{:S(2)}, u32[]{:S(2)}) collective-permute-start(bf16[256,2048]{1,0:T(8,128)(2,1)S(1)} %fusion.8), channel_id=1, source_target_pairs={{0,1},{1,0},{2,3},{3,2},{4,5},{5,4},{6,7},{7,6},{8,9},{9,8},{10,11... | collective-permute-start | bytes 3145736 | tf_op jit(solution)/shard_map/ppermute | solution.py:29
  154.5 9.3 %collective-permute-start.22 = (bf16[64,2048]{1,0:T(8,128)(2,1)S(1)}, bf16[64,2048]{1,0:T(8,128)(2,1)S(1)}, u32[]{:S(2)}, u32[]{:S(2)}) collective-permute-start(bf16[64,2048]{1,0:T(8,128)(2,1)S(1)} %get-tuple-element.15), channel_id=1, source_target_pairs={{0,6},{2,0},{4,2},{6,4},{1,7},{3,1},{5,3},{7,5},{8,14},{10,8},{12,... | collective-permute-start | bytes 786440 | tf_op jit(solution)/shard_map/ppermute | solution.py:65
  155.4 10.7 %collective-permute-start.21 = (bf16[64,2048]{1,0:T(8,128)(2,1)S(1)}, bf16[64,2048]{1,0:T(8,128)(2,1)S(1)}, u32[]{:S(2)}, u32[]{:S(2)}) collective-permute-start(bf16[64,2048]{1,0:T(8,128)(2,1)S(1)} %get-tuple-element.16), channel_id=1, source_target_pairs={{0,4},{2,6},{4,0},{6,2},{1,5},{3,7},{5,1},{7,3},{8,12},{10,14},{12... | collective-permute-start | bytes 786440 | tf_op jit(solution)/shard_map/ppermute | solution.py:65
  157.1 13.7 %collective-permute-start.20 = (bf16[64,2048]{1,0:T(8,128)(2,1)S(1)}, bf16[64,2048]{1,0:T(8,128)(2,1)S(1)}, u32[]{:S(2)}, u32[]{:S(2)}) collective-permute-start(bf16[64,2048]{1,0:T(8,128)(2,1)S(1)} %get-tuple-element.14), channel_id=1, source_target_pairs={{0,2},{2,4},{4,6},{6,0},{1,3},{3,5},{5,7},{7,1},{8,10},{10,12},{12... | collective-permute-start | bytes 786440 | tf_op jit(solution)/shard_map/ppermute | solution.py:65
  171.7 15.7 %all-to-all-start.4 = ((bf16[8,8,2048]{2,1,0:T(8,128)(2,1)}), bf16[8,8,2048]{2,1,0:T(8,128)(2,1)S(1)}, u32[]{:S(2)}, u32[]{:S(2)}) async-start(bf16[8,8,2048]{2,1,0:T(8,128)(2,1)} %fusion.39), calls=%async_computation.4 | async-start | bytes 524288 | tf_op jit(solution)/shard_map/all_to_all | solution.py:60
  175.1 13.7 %collective-permute-start.18 = (f32[4,2048]{1,0:T(4,128)S(1)}, f32[4,2048]{1,0:T(4,128)S(1)}, u32[]{:S(2)}, u32[]{:S(2)}) collective-permute-start(f32[4,2048]{1,0:T(4,128)S(1)} %get-tuple-element.22), channel_id=1, source_target_pairs={{0,1},{1,0},{2,3},{3,2},{4,5},{5,4},{6,7},{7,6},{8,9},{9,8},{10,11... | collective-permute-start | bytes 98312 | tf_op jit(solution)/shard_map/ppermute | solution.py:29
  187.4 1.5 collective-permute-start.23
  (3 other events, 74.1 us)

commit v3 on v2

--- a/solution.py
+++ b/solution.py
@@ -76,12 +76,11 @@
     spread = jnp.broadcast_to(block[None], (lax.axis_size("z"), *block.shape))
     plane = exchange(spread, "z").reshape(-1, block.shape[-1])
     got = [along_y(plane, -k) for k in range(1, lax.axis_size("y"))]
-    mine = jnp.concatenate([plane, *got], axis=0)
-    return mine, swap(mine)
+    theirs = [swap(x) for x in (plane, *got)]
+    return [lax.optimization_barrier(jnp.concatenate(x, axis=0)) for x in ([plane, *got], theirs)]
 
 
-def both_halves(mine, theirs, weight, core):
-    own, other = halves(weight, core, 0)
+def both_halves(mine, theirs, own, other):
     first = lax.optimization_barrier(mm(mine, own))
     return first + mm(theirs, other)
 
@@ -122,7 +121,7 @@
     residual8 = chip_rows(residual, core).astype(F32)
     gain8 = halves(final_gain[None, :], core, 1)[0]
 
-    gu = both_halves(mine, theirs, gate_up, core)
+    gu = both_halves(mine, theirs, *halves(gate_up, core, 0))
     hid = gate_weight.shape[1]
     activated = (jax.nn.silu(gu[:, :hid]) * gu[:, hid:]).astype(BF)
     down_own, down_other = halves(down_weight, core, 1)
@@ -136,7 +135,8 @@
     hidden = core_rows(hidden8, core)
     scale = rms_scale(hidden)
 
-    logits = both_halves(mine, theirs, head_weight, core)
+    head_own, head_other = lax.optimization_barrier(halves(head_weight, core, 0))
+    logits = both_halves(mine, theirs, head_own, head_other)
     positive = jnp.maximum(logits, 0.0)
     weights = jnp.log1p(positive)
     powered = valid[:, None] * weights**4
@@ -159,7 +159,6 @@
     entropy = jnp.log(total) - spread / total
     slope_mass = jnp.log(total) - log_smooth.reshape(-1)
     slope_logit = lax.optimization_barrier((slope * slope_mass[None, :]).astype(BF))
-    head_own, head_other = halves(head_weight, core, 0)
     other = mm_t(slope_logit, head_other).astype(BF)
     own = lax.optimization_barrier(mm_t(slope_logit, head_own))
     slope_normed = core_rows(scatter(own, other), core)

time: 194 us -> 192 us (0.990)
  the two profiles are of different devices: /device:TPU:2 before, /device:TPU:31 now
where the time goes in v3:
time: 192 us; the launch traced here: 191 us
  waiting for transfers between devices  90.6 us (47%)
  starting transfers between devices  60.8 us (32%)
  local copies, waits for them, and re-layouts  14.4 us (8%)
  matrix products  14.2 us (7%)
  other arithmetic  6.92 us (4%)
  between operations  4.27 us (2%)
    ppermute x12, waiting for transfers between devices, along_y(): return lax.ppermute(x, 'y', [(i, (i + k) % n) for i in range(n)])  41 us
    all_to_all x5, waiting for transfers between devices, exchange(): return lax.all_to_all(x, axes, 0, 0)  40.7 us
    all_to_all x5, starting transfers between devices, exchange(): return lax.all_to_all(x, axes, 0, 0)  26.5 us
    ppermute x15, starting transfers between devices, swap(): return lax.ppermute(x, 'c', [(0, 1), (1, 0)])  19.7 us
    ppermute x12, starting transfers between devices, along_y(): return lax.ppermute(x, 'y', [(i, (i + k) % n) for i in range(n)])  11.6 us
    dynamic_slice x4, local copies, waits for them, and re-layouts, halves(): other = lax.dynamic_slice_in_dim(x, (1 - core) * size, size, axis)  7.79 us
    dot_general x6, matrix products, mm(): return jnp.dot(a, b, preferred_element_type=F32)  7.14 us
    ppermute x15, waiting for transfers between devices, swap(): return lax.ppermute(x, 'c', [(0, 1), (1, 0)])  5.22 us
  transfers between devices with their start and end apart: 35, of which 22 were waited for; matrix products, arithmetic and copies ran while one was open for 10% of the time, Pallas kernels for 0%

profile of v3, /device:TPU:31, one launch (start us, length us, event | category | flops | bytes accessed | tf_op | source)
XLA Modules:
  0.0 191.1 jit_solution(3536460148375536794)
XLA Ops:
  4.9 8.2 %all-to-all-start = ((bf16[8,8,2048]{2,1,0:T(8,128)(2,1)}), bf16[8,8,2048]{2,1,0:T(8,128)(2,1)S(1)}, u32[]{:S(2)}, u32[]{:S(2)}) async-start(bf16[8,8,2048]{2,1,0:T(8,128)(2,1)} %broadcast_in_dim.55), calls=%async_computation | async-start | bytes 524288 | tf_op jit(solution)/shard_map/all_to_all | solution.py:60
  14.5 9.8 %all-to-all-done = bf16[8,8,2048]{2,1,0:T(8,128)(2,1)S(1)} async-done(((bf16[8,8,2048]{2,1,0:T(8,128)(2,1)}), bf16[8,8,2048]{2,1,0:T(8,128)(2,1)S(1)}, u32[]{:S(2)}, u32[]{:S(2)}) %all-to-all-start) | async-done | bytes 262176 | tf_op jit(solution)/shard_map/all_to_all | solution.py:60
  25.4 1.9 collective-permute-start.4
  28.8 2.5 %collective-permute-start.5 = (bf16[64,2048]{1,0:T(8,128)(2,1)S(1)}, bf16[64,2048]{1,0:T(8,128)(2,1)S(1)}, u32[]{:S(2)}, u32[]{:S(2)}) collective-permute-start(bf16[64,2048]{1,0:T(8,128)(2,1)S(1)} %bitcast.51), channel_id=1, source_target_pairs={{0,1},{1,0},{2,3},{3,2},{4,5},{5,4},{6,7},{7,6},{8,9},{9,8},{10,11... | collective-permute-start | bytes 786440 | tf_op jit(solution)/shard_map/ppermute | solution.py:29
  31.3 2.0 %collective-permute-done.2 = bf16[64,2048]{1,0:T(8,128)(2,1)S(1)} collective-permute-done((bf16[64,2048]{1,0:T(8,128)(2,1)S(1)}, bf16[64,2048]{1,0:T(8,128)(2,1)S(1)}, u32[]{:S(2)}, u32[]{:S(2)}) %collective-permute-start.2) | collective-permute-done | bytes 262176 | tf_op jit(solution)/shard_map/ppermute | solution.py:65
  33.4 6.5 %collective-permute-start.6 = (bf16[64,2048]{1,0:T(8,128)(2,1)S(1)}, bf16[64,2048]{1,0:T(8,128)(2,1)S(1)}, u32[]{:S(2)}, u32[]{:S(2)}) collective-permute-start(bf16[64,2048]{1,0:T(8,128)(2,1)S(1)} %collective-permute-done.2), channel_id=1, source_target_pairs={{0,1},{1,0},{2,3},{3,2},{4,5},{5,4},{6,7},{7,6},{8,9},{9,8},{10,11... | collective-permute-start | bytes 786440 | tf_op jit(solution)/shard_map/ppermute | solution.py:29
  43.8 1.9 collective-permute-done.9
  45.8 2.3 %collective-permute-start.10 = (bf16[64,2048]{1,0:T(8,128)(2,1)S(1)}, bf16[64,2048]{1,0:T(8,128)(2,1)S(1)}, u32[]{:S(2)}, u32[]{:S(2)}) collective-permute-start(bf16[64,2048]{1,0:T(8,128)(2,1)S(1)} %get-tuple-element.23), channel_id=1, source_target_pairs={{0,2},{2,4},{4,6},{6,0},{1,3},{3,5},{5,7},{7,1},{8,10},{10,12},{12... | collective-permute-start | bytes 786440 | tf_op jit(solution)/shard_map/ppermute | solution.py:65
  48.8 5.1 %collective-permute-done.10 = bf16[64,2048]{1,0:T(8,128)(2,1)S(1)} collective-permute-done((bf16[64,2048]{1,0:T(8,128)(2,1)S(1)}, bf16[64,2048]{1,0:T(8,128)(2,1)S(1)}, u32[]{:S(2)}, u32[]{:S(2)}) %collective-permute-start.10) | collective-permute-done | bytes 262176 | tf_op jit(solution)/shard_map/ppermute | solution.py:65
  53.9 3.0 %collective-permute-done.11 = bf16[64,2048]{1,0:T(8,128)(2,1)S(1)} collective-permute-done((bf16[64,2048]{1,0:T(8,128)(2,1)S(1)}, bf16[64,2048]{1,0:T(8,128)(2,1)S(1)}, u32[]{:S(2)}, u32[]{:S(2)}) %collective-permute-start.11) | collective-permute-done | bytes 262176 | tf_op jit(solution)/shard_map/ppermute | solution.py:65
  56.9 6.0 %collective-permute-done.12 = bf16[64,2048]{1,0:T(8,128)(2,1)S(1)} collective-permute-done((bf16[64,2048]{1,0:T(8,128)(2,1)S(1)}, bf16[64,2048]{1,0:T(8,128)(2,1)S(1)}, u32[]{:S(2)}, u32[]{:S(2)}) %collective-permute-start.12) | collective-permute-done | bytes 262176 | tf_op jit(solution)/shard_map/ppermute | solution.py:65
  63.7 3.4 %all-to-all-start.1 = ((bf16[8,8,2048]{2,1,0:T(8,128)(2,1)}), bf16[8,8,2048]{2,1,0:T(8,128)(2,1)S(1)}, u32[]{:S(2)}, u32[]{:S(2)}) async-start(bf16[8,8,2048]{2,1,0:T(8,128)(2,1)} %fusion.27), calls=%async_computation.1 | async-start | bytes 524288 | tf_op jit(solution)/shard_map/all_to_all | solution.py:60
  68.3 7.7 %constant_dynamic-slice_fusion.4 = (bf16[2048,1024]{1,0:T(8,128)(2,1)}, bf16[2048,1024]{1,0:T(8,128)(2,1)}) fusion(bf16[4096,1024]{1,0:T(8,128)(2,1)} %param.15, s32[]{:T(128)S(6)} %select_n.71, s32[]{:T(128)} %select_n.70), kind=kLoop, calls=%fused_computation.90 | loop fusion | bytes 16777224 | tf_op jit(solution)/shard_map/dynamic_slice | solution.py:43
  76.0 1.8 all-to-all-done.1
  78.0 2.1 %collective-permute-start.13 = (f32[8,1]{0,1:T(1,128)S(1)}, f32[8,1]{0,1:T(1,128)S(1)}, u32[]{:S(2)}, u32[]{:S(2)}) collective-permute-start(f32[8,1]{0,1:T(1,128)S(1)} %bitcast.60), channel_id=1, source_target_pairs={{0,1},{1,0},{2,3},{3,2},{4,5},{5,4},{6,7},{7,6},{8,9},{9,8},{10,11... | collective-permute-start | bytes 104 | tf_op jit(solution)/shard_map/ppermute | solution.py:29
  81.8 3.4 %all-to-all-start.2 = ((bf16[8,8,2048]{2,1,0:T(8,128)(2,1)}), bf16[8,8,2048]{2,1,0:T(8,128)(2,1)S(1)}, u32[]{:S(2)}, u32[]{:S(2)}) async-start(bf16[8,8,2048]{2,1,0:T(8,128)(2,1)} %broadcast_in_dim.57), calls=%async_computation.2 | async-start | bytes 524288 | tf_op jit(solution)/shard_map/all_to_all | solution.py:60
  87.1 10.4 %all-to-all-done.2 = bf16[8,8,2048]{2,1,0:T(8,128)(2,1)S(1)} async-done(((bf16[8,8,2048]{2,1,0:T(8,128)(2,1)}), bf16[8,8,2048]{2,1,0:T(8,128)(2,1)S(1)}, u32[]{:S(2)}, u32[]{:S(2)}) %all-to-all-start.2) | async-done | bytes 262176 | tf_op jit(solution)/shard_map/all_to_all | solution.py:60
  101.7 10.0 %collective-permute-done.14 = bf16[64,2048]{1,0:T(8,128)(2,1)S(1)} collective-permute-done((bf16[64,2048]{1,0:T(8,128)(2,1)S(1)}, bf16[64,2048]{1,0:T(8,128)(2,1)S(1)}, u32[]{:S(2)}, u32[]{:S(2)}) %collective-permute-start.14) | collective-permute-done | bytes 262176 | tf_op jit(solution)/shard_map/ppermute | solution.py:65
  112.2 1.7 collective-permute-start.18
  114.4 3.6 %fusion.49 = f32[256,1024]{1,0:T(8,128)S(1)} fusion(bf16[256,2048]{1,0:T(8,128)(2,1)S(1)} %pad_maximum_fusion.2, bf16[2048,1024]{1,0:T(8,128)(2,1)} %get-tuple-element.5), kind=kOutput, calls=%fused_computation.118 | convolution fusion | flops 1073741824 | bytes 6291456 | tf_op jit(solution)/shard_map/dot_general | solution.py:33
  118.1 1.8 fusion.4
  122.5 1.8 collective-permute-start.22
  125.3 2.6 %collective-permute-done.23 = f32[8,128]{1,0:T(8,128)S(1)} collective-permute-done((f32[8,128]{1,0:T(8,128)S(1)}, f32[8,128]{1,0:T(8,128)S(1)}, u32[]{:S(2)}, u32[]{:S(2)}) %collective-permute-start.23) | collective-permute-done | bytes 4128 | tf_op jit(solution)/shard_map/ppermute | solution.py:147
  128.7 8.1 %all-to-all-start.3 = ((f32[64,2,128]{2,1,0:T(2,128)}), f32[64,2,128]{2,1,0:T(2,128)S(1)}, u32[]{:S(2)}, u32[]{:S(2)}) async-start(f32[64,2,128]{2,1,0:T(2,128)} %broadcast_in_dim.58), calls=%async_computation.3 | async-start | bytes 131072 | tf_op jit(solution)/shard_map/all_to_all | solution.py:60
  137.4 7.5 %all-to-all-done.3 = f32[64,2,128]{2,1,0:T(2,128)S(1)} async-done(((f32[64,2,128]{2,1,0:T(2,128)}), f32[64,2,128]{2,1,0:T(2,128)S(1)}, u32[]{:S(2)}, u32[]{:S(2)}) %all-to-all-start.3) | async-done | bytes 65568 | tf_op jit(solution)/shard_map/all_to_all | solution.py:60
  146.5 3.6 %convolution_convert_fusion.1 = bf16[256,2048]{1,0:T(8,128)(2,1)S(1)} fusion(bf16[256,1024]{1,0:T(8,128)(2,1)S(1)} %multiply_convert_fusion, bf16[2048,1024]{1,0:T(8,128)(2,1)} %get-tuple-element.6), kind=kOutput, calls=%fused_computation.1 | convolution fusion | flops 1074266112 | bytes 5767168 | tf_op jit(solution)/shard_map/dot_general | solution.py:37
  153.1 2.1 %collective-permute-start.26 = (bf16[64,2048]{1,0:T(8,128)(2,1)S(1)}, bf16[64,2048]{1,0:T(8,128)(2,1)S(1)}, u32[]{:S(2)}, u32[]{:S(2)}) collective-permute-start(bf16[64,2048]{1,0:T(8,128)(2,1)S(1)} %get-tuple-element.20), channel_id=1, source_target_pairs={{0,2},{2,4},{4,6},{6,0},{1,3},{3,5},{5,7},{7,1},{8,10},{10,12},{12... | collective-permute-start | bytes 786440 | tf_op jit(solution)/shard_map/ppermute | solution.py:65
  156.0 4.8 %collective-permute-done.26 = bf16[64,2048]{1,0:T(8,128)(2,1)S(1)} collective-permute-done((bf16[64,2048]{1,0:T(8,128)(2,1)S(1)}, bf16[64,2048]{1,0:T(8,128)(2,1)S(1)}, u32[]{:S(2)}, u32[]{:S(2)}) %collective-permute-start.26) | collective-permute-done | bytes 262176 | tf_op jit(solution)/shard_map/ppermute | solution.py:65
  160.9 3.1 %collective-permute-done.27 = bf16[64,2048]{1,0:T(8,128)(2,1)S(1)} collective-permute-done((bf16[64,2048]{1,0:T(8,128)(2,1)S(1)}, bf16[64,2048]{1,0:T(8,128)(2,1)S(1)}, u32[]{:S(2)}, u32[]{:S(2)}) %collective-permute-start.27) | collective-permute-done | bytes 262176 | tf_op jit(solution)/shard_map/ppermute | solution.py:65
  163.9 6.6 %collective-permute-done.28 = bf16[64,2048]{1,0:T(8,128)(2,1)S(1)} collective-permute-done((bf16[64,2048]{1,0:T(8,128)(2,1)S(1)}, bf16[64,2048]{1,0:T(8,128)(2,1)S(1)}, u32[]{:S(2)}, u32[]{:S(2)}) %collective-permute-start.28) | collective-permute-done | bytes 262176 | tf_op jit(solution)/shard_map/ppermute | solution.py:65
  171.4 3.4 %all-to-all-start.4 = ((bf16[8,8,2048]{2,1,0:T(8,128)(2,1)}), bf16[8,8,2048]{2,1,0:T(8,128)(2,1)S(1)}, u32[]{:S(2)}, u32[]{:S(2)}) async-start(bf16[8,8,2048]{2,1,0:T(8,128)(2,1)} %fusion.28), calls=%async_computation.4 | async-start | bytes 524288 | tf_op jit(solution)/shard_map/all_to_all | solution.py:60
  175.4 11.2 %all-to-all-done.4 = bf16[8,8,2048]{2,1,0:T(8,128)(2,1)S(1)} async-done(((bf16[8,8,2048]{2,1,0:T(8,128)(2,1)}), bf16[8,8,2048]{2,1,0:T(8,128)(2,1)S(1)}, u32[]{:S(2)}, u32[]{:S(2)}) %all-to-all-start.4) | async-done | bytes 262176 | tf_op jit(solution)/shard_map/all_to_all | solution.py:60
  (116 shorter events, 36.9 us)
Async XLA Ops:
  4.9 19.4 %all-to-all-start = ((bf16[8,8,2048]{2,1,0:T(8,128)(2,1)}), bf16[8,8,2048]{2,1,0:T(8,128)(2,1)S(1)}, u32[]{:S(2)}, u32[]{:S(2)}) async-start(bf16[8,8,2048]{2,1,0:T(8,128)(2,1)} %broadcast_in_dim.55), calls=%async_computation | async-start | bytes 524288 | tf_op jit(solution)/shard_map/all_to_all | solution.py:60
  24.3 9.1 %collective-permute-start.2 = (bf16[64,2048]{1,0:T(8,128)(2,1)S(1)}, bf16[64,2048]{1,0:T(8,128)(2,1)S(1)}, u32[]{:S(2)}, u32[]{:S(2)}) collective-permute-start(bf16[64,2048]{1,0:T(8,128)(2,1)S(1)} %bitcast.48), channel_id=1, source_target_pairs={{0,6},{2,0},{4,2},{6,4},{1,7},{3,1},{5,3},{7,5},{8,14},{10,8},{12,... | collective-permute-start | bytes 786440 | tf_op jit(solution)/shard_map/ppermute | solution.py:65
  24.8 15.1 %collective-permute-start.3 = (bf16[64,2048]{1,0:T(8,128)(2,1)S(1)}, bf16[64,2048]{1,0:T(8,128)(2,1)S(1)}, u32[]{:S(2)}, u32[]{:S(2)}) collective-permute-start(bf16[64,2048]{1,0:T(8,128)(2,1)S(1)} %bitcast.49), channel_id=1, source_target_pairs={{0,4},{2,6},{4,0},{6,2},{1,5},{3,7},{5,1},{7,3},{8,12},{10,14},{12... | collective-permute-start | bytes 786440 | tf_op jit(solution)/shard_map/ppermute | solution.py:65
  25.4 14.4 %collective-permute-start.4 = (bf16[64,2048]{1,0:T(8,128)(2,1)S(1)}, bf16[64,2048]{1,0:T(8,128)(2,1)S(1)}, u32[]{:S(2)}, u32[]{:S(2)}) collective-permute-start(bf16[64,2048]{1,0:T(8,128)(2,1)S(1)} %bitcast.50), channel_id=1, source_target_pairs={{0,2},{2,4},{4,6},{6,0},{1,3},{3,5},{5,7},{7,1},{8,10},{10,12},{12... | collective-permute-start | bytes 786440 | tf_op jit(solution)/shard_map/ppermute | solution.py:65
  28.8 12.2 %collective-permute-start.5 = (bf16[64,2048]{1,0:T(8,128)(2,1)S(1)}, bf16[64,2048]{1,0:T(8,128)(2,1)S(1)}, u32[]{:S(2)}, u32[]{:S(2)}) collective-permute-start(bf16[64,2048]{1,0:T(8,128)(2,1)S(1)} %bitcast.51), channel_id=1, source_target_pairs={{0,1},{1,0},{2,3},{3,2},{4,5},{5,4},{6,7},{7,6},{8,9},{9,8},{10,11... | collective-permute-start | bytes 786440 | tf_op jit(solution)/shard_map/ppermute | solution.py:29
  33.4 7.7 %collective-permute-start.6 = (bf16[64,2048]{1,0:T(8,128)(2,1)S(1)}, bf16[64,2048]{1,0:T(8,128)(2,1)S(1)}, u32[]{:S(2)}, u32[]{:S(2)}) collective-permute-start(bf16[64,2048]{1,0:T(8,128)(2,1)S(1)} %collective-permute-done.2), channel_id=1, source_target_pairs={{0,1},{1,0},{2,3},{3,2},{4,5},{5,4},{6,7},{7,6},{8,9},{9,8},{10,11... | collective-permute-start | bytes 786440 | tf_op jit(solution)/shard_map/ppermute | solution.py:29
  42.9 2.7 %collective-permute-start.9 = (bf16[256,2048]{1,0:T(8,128)(2,1)S(1)}, bf16[256,2048]{1,0:T(8,128)(2,1)S(1)}, u32[]{:S(2)}, u32[]{:S(2)}) collective-permute-start(bf16[256,2048]{1,0:T(8,128)(2,1)S(1)} %convolution_convert_fusion), channel_id=1, source_target_pairs={{0,1},{1,0},{2,3},{3,2},{4,5},{5,4},{6,7},{7,6},{8,9},{9,8},{10,11... | collective-permute-start | bytes 3145736 | tf_op jit(solution)/shard_map/ppermute | solution.py:29
  45.8 8.1 %collective-permute-start.10 = (bf16[64,2048]{1,0:T(8,128)(2,1)S(1)}, bf16[64,2048]{1,0:T(8,128)(2,1)S(1)}, u32[]{:S(2)}, u32[]{:S(2)}) collective-permute-start(bf16[64,2048]{1,0:T(8,128)(2,1)S(1)} %get-tuple-element.23), channel_id=1, source_target_pairs={{0,2},{2,4},{4,6},{6,0},{1,3},{3,5},{5,7},{7,1},{8,10},{10,12},{12... | collective-permute-start | bytes 786440 | tf_op jit(solution)/shard_map/ppermute | solution.py:65
  48.1 8.8 %collective-permute-start.11 = (bf16[64,2048]{1,0:T(8,128)(2,1)S(1)}, bf16[64,2048]{1,0:T(8,128)(2,1)S(1)}, u32[]{:S(2)}, u32[]{:S(2)}) collective-permute-start(bf16[64,2048]{1,0:T(8,128)(2,1)S(1)} %get-tuple-element.25), channel_id=1, source_target_pairs={{0,4},{2,6},{4,0},{6,2},{1,5},{3,7},{5,1},{7,3},{8,12},{10,14},{12... | collective-permute-start | bytes 786440 | tf_op jit(solution)/shard_map/ppermute | solution.py:65
  48.1 14.8 %collective-permute-start.12 = (bf16[64,2048]{1,0:T(8,128)(2,1)S(1)}, bf16[64,2048]{1,0:T(8,128)(2,1)S(1)}, u32[]{:S(2)}, u32[]{:S(2)}) collective-permute-start(bf16[64,2048]{1,0:T(8,128)(2,1)S(1)} %get-tuple-element.24), channel_id=1, source_target_pairs={{0,6},{2,0},{4,2},{6,4},{1,7},{3,1},{5,3},{7,5},{8,14},{10,8},{12,... | collective-permute-start | bytes 786440 | tf_op jit(solution)/shard_map/ppermute | solution.py:65
  63.7 14.1 %all-to-all-start.1 = ((bf16[8,8,2048]{2,1,0:T(8,128)(2,1)}), bf16[8,8,2048]{2,1,0:T(8,128)(2,1)S(1)}, u32[]{:S(2)}, u32[]{:S(2)}) async-start(bf16[8,8,2048]{2,1,0:T(8,128)(2,1)} %fusion.27), calls=%async_computation.1 | async-start | bytes 524288 | tf_op jit(solution)/shard_map/all_to_all | solution.py:60
  67.2 10.7 %collective-permute-start = (bf16[4,2048]{1,0:T(4,128)(2,1)S(1)}, bf16[4,2048]{1,0:T(4,128)(2,1)S(1)}, u32[]{:S(2)}, u32[]{:S(2)}) collective-permute-start(bf16[4,2048]{1,0:T(4,128)(2,1)S(1)} %get-tuple-element.30), channel_id=1, source_target_pairs={{0,1},{1,0},{2,3},{3,2},{4,5},{5,4},{6,7},{7,6},{8,9},{9,8},{10,11... | collective-permute-start | bytes 49160 | tf_op jit(solution)/shard_map/ppermute | solution.py:29
  78.0 3.0 %collective-permute-start.13 = (f32[8,1]{0,1:T(1,128)S(1)}, f32[8,1]{0,1:T(1,128)S(1)}, u32[]{:S(2)}, u32[]{:S(2)}) collective-permute-start(f32[8,1]{0,1:T(1,128)S(1)} %bitcast.60), channel_id=1, source_target_pairs={{0,1},{1,0},{2,3},{3,2},{4,5},{5,4},{6,7},{7,6},{8,9},{9,8},{10,11... | collective-permute-start | bytes 104 | tf_op jit(solution)/shard_map/ppermute | solution.py:29
  81.8 15.7 %all-to-all-start.2 = ((bf16[8,8,2048]{2,1,0:T(8,128)(2,1)}), bf16[8,8,2048]{2,1,0:T(8,128)(2,1)S(1)}, u32[]{:S(2)}, u32[]{:S(2)}) async-start(bf16[8,8,2048]{2,1,0:T(8,128)(2,1)} %broadcast_in_dim.57), calls=%async_computation.2 | async-start | bytes 524288 | tf_op jit(solution)/shard_map/all_to_all | solution.py:60
  97.5 14.2 %collective-permute-start.14 = (bf16[64,2048]{1,0:T(8,128)(2,1)S(1)}, bf16[64,2048]{1,0:T(8,128)(2,1)S(1)}, u32[]{:S(2)}, u32[]{:S(2)}) collective-permute-start(bf16[64,2048]{1,0:T(8,128)(2,1)S(1)} %bitcast.43), channel_id=1, source_target_pairs={{0,6},{2,0},{4,2},{6,4},{1,7},{3,1},{5,3},{7,5},{8,14},{10,8},{12,... | collective-permute-start | bytes 786440 | tf_op jit(solution)/shard_map/ppermute | solution.py:65
  97.5 14.2 %collective-permute-start.15 = (bf16[64,2048]{1,0:T(8,128)(2,1)S(1)}, bf16[64,2048]{1,0:T(8,128)(2,1)S(1)}, u32[]{:S(2)}, u32[]{:S(2)}) collective-permute-start(bf16[64,2048]{1,0:T(8,128)(2,1)S(1)} %bitcast.44), channel_id=1, source_target_pairs={{0,4},{2,6},{4,0},{6,2},{1,5},{3,7},{5,1},{7,3},{8,12},{10,14},{12... | collective-permute-start | bytes 786440 | tf_op jit(solution)/shard_map/ppermute | solution.py:65
  99.1 13.0 %collective-permute-start.16 = (bf16[64,2048]{1,0:T(8,128)(2,1)S(1)}, bf16[64,2048]{1,0:T(8,128)(2,1)S(1)}, u32[]{:S(2)}, u32[]{:S(2)}) collective-permute-start(bf16[64,2048]{1,0:T(8,128)(2,1)S(1)} %bitcast.45), channel_id=1, source_target_pairs={{0,2},{2,4},{4,6},{6,0},{1,3},{3,5},{5,7},{7,1},{8,10},{10,12},{12... | collective-permute-start | bytes 786440 | tf_op jit(solution)/shard_map/ppermute | solution.py:65
  100.4 17.6 %collective-permute-start.17 = (bf16[64,2048]{1,0:T(8,128)(2,1)S(1)}, bf16[64,2048]{1,0:T(8,128)(2,1)S(1)}, u32[]{:S(2)}, u32[]{:S(2)}) collective-permute-start(bf16[64,2048]{1,0:T(8,128)(2,1)S(1)} %bitcast.46), channel_id=1, source_target_pairs={{0,1},{1,0},{2,3},{3,2},{4,5},{5,4},{6,7},{7,6},{8,9},{9,8},{10,11... | collective-permute-start | bytes 786440 | tf_op jit(solution)/shard_map/ppermute | solution.py:29
  112.2 5.8 %collective-permute-start.18 = (bf16[64,2048]{1,0:T(8,128)(2,1)S(1)}, bf16[64,2048]{1,0:T(8,128)(2,1)S(1)}, u32[]{:S(2)}, u32[]{:S(2)}) collective-permute-start(bf16[64,2048]{1,0:T(8,128)(2,1)S(1)} %collective-permute-done.14), channel_id=1, source_target_pairs={{0,1},{1,0},{2,3},{3,2},{4,5},{5,4},{6,7},{7,6},{8,9},{9,8},{10,11... | collective-permute-start | bytes 786440 | tf_op jit(solution)/shard_map/ppermute | solution.py:29
  113.9 4.2 %collective-permute-start.19 = (bf16[64,2048]{1,0:T(8,128)(2,1)S(1)}, bf16[64,2048]{1,0:T(8,128)(2,1)S(1)}, u32[]{:S(2)}, u32[]{:S(2)}) collective-permute-start(bf16[64,2048]{1,0:T(8,128)(2,1)S(1)} %collective-permute-done.15), channel_id=1, source_target_pairs={{0,1},{1,0},{2,3},{3,2},{4,5},{5,4},{6,7},{7,6},{8,9},{9,8},{10,11... | collective-permute-start | bytes 786440 | tf_op jit(solution)/shard_map/ppermute | solution.py:29
  114.0 4.1 %collective-permute-start.20 = (bf16[64,2048]{1,0:T(8,128)(2,1)S(1)}, bf16[64,2048]{1,0:T(8,128)(2,1)S(1)}, u32[]{:S(2)}, u32[]{:S(2)}) collective-permute-start(bf16[64,2048]{1,0:T(8,128)(2,1)S(1)} %collective-permute-done.16), channel_id=1, source_target_pairs={{0,1},{1,0},{2,3},{3,2},{4,5},{5,4},{6,7},{7,6},{8,9},{9,8},{10,11... | collective-permute-start | bytes 786440 | tf_op jit(solution)/shard_map/ppermute | solution.py:29
  121.4 4.0 %collective-permute-start.21 = (f32[8,128]{1,0:T(8,128)S(1)}, f32[8,128]{1,0:T(8,128)S(1)}, u32[]{:S(2)}, u32[]{:S(2)}) collective-permute-start(f32[8,128]{1,0:T(8,128)S(1)} %bitcast.55), channel_id=1, source_target_pairs={{0,128},{64,192},{128,0},{192,64},{1,129},{65,193},{129,1},{193,65... | collective-permute-start | bytes 12296 | tf_op jit(solution)/shard_map/ppermute | solution.py:147
  122.5 2.8 %collective-permute-start.22 = (f32[8,128]{1,0:T(8,128)S(1)}, f32[8,128]{1,0:T(8,128)S(1)}, u32[]{:S(2)}, u32[]{:S(2)}) collective-permute-start(f32[8,128]{1,0:T(8,128)S(1)} %bitcast.56), channel_id=1, source_target_pairs={{0,64},{64,128},{128,192},{192,0},{1,65},{65,129},{129,193},{193,1... | collective-permute-start | bytes 12296 | tf_op jit(solution)/shard_map/ppermute | solution.py:147
  124.3 3.7 %collective-permute-start.23 = (f32[8,128]{1,0:T(8,128)S(1)}, f32[8,128]{1,0:T(8,128)S(1)}, u32[]{:S(2)}, u32[]{:S(2)}) collective-permute-start(f32[8,128]{1,0:T(8,128)S(1)} %bitcast.57), channel_id=1, source_target_pairs={{0,192},{64,0},{128,64},{192,128},{1,193},{65,1},{129,65},{193,129... | collective-permute-start | bytes 12296 | tf_op jit(solution)/shard_map/ppermute | solution.py:147
  128.7 16.2 %all-to-all-start.3 = ((f32[64,2,128]{2,1,0:T(2,128)}), f32[64,2,128]{2,1,0:T(2,128)S(1)}, u32[]{:S(2)}, u32[]{:S(2)}) async-start(f32[64,2,128]{2,1,0:T(2,128)} %broadcast_in_dim.58), calls=%async_computation.3 | async-start | bytes 131072 | tf_op jit(solution)/shard_map/all_to_all | solution.py:60
  150.1 2.8 %collective-permute-start.25 = (bf16[256,2048]{1,0:T(8,128)(2,1)S(1)}, bf16[256,2048]{1,0:T(8,128)(2,1)S(1)}, u32[]{:S(2)}, u32[]{:S(2)}) collective-permute-start(bf16[256,2048]{1,0:T(8,128)(2,1)S(1)} %convolution_convert_fusion.1), channel_id=1, source_target_pairs={{0,1},{1,0},{2,3},{3,2},{4,5},{5,4},{6,7},{7,6},{8,9},{9,8},{10,11... | collective-permute-start | bytes 3145736 | tf_op jit(solution)/shard_map/ppermute | solution.py:29
  153.1 7.8 %collective-permute-start.26 = (bf16[64,2048]{1,0:T(8,128)(2,1)S(1)}, bf16[64,2048]{1,0:T(8,128)(2,1)S(1)}, u32[]{:S(2)}, u32[]{:S(2)}) collective-permute-start(bf16[64,2048]{1,0:T(8,128)(2,1)S(1)} %get-tuple-element.20), channel_id=1, source_target_pairs={{0,2},{2,4},{4,6},{6,0},{1,3},{3,5},{5,7},{7,1},{8,10},{10,12},{12... | collective-permute-start | bytes 786440 | tf_op jit(solution)/shard_map/ppermute | solution.py:65
  155.2 8.8 %collective-permute-start.27 = (bf16[64,2048]{1,0:T(8,128)(2,1)S(1)}, bf16[64,2048]{1,0:T(8,128)(2,1)S(1)}, u32[]{:S(2)}, u32[]{:S(2)}) collective-permute-start(bf16[64,2048]{1,0:T(8,128)(2,1)S(1)} %get-tuple-element.22), channel_id=1, source_target_pairs={{0,4},{2,6},{4,0},{6,2},{1,5},{3,7},{5,1},{7,3},{8,12},{10,14},{12... | collective-permute-start | bytes 786440 | tf_op jit(solution)/shard_map/ppermute | solution.py:65
  155.6 14.9 %collective-permute-start.28 = (bf16[64,2048]{1,0:T(8,128)(2,1)S(1)}, bf16[64,2048]{1,0:T(8,128)(2,1)S(1)}, u32[]{:S(2)}, u32[]{:S(2)}) collective-permute-start(bf16[64,2048]{1,0:T(8,128)(2,1)S(1)} %get-tuple-element.21), channel_id=1, source_target_pairs={{0,6},{2,0},{4,2},{6,4},{1,7},{3,1},{5,3},{7,5},{8,14},{10,8},{12,... | collective-permute-start | bytes 786440 | tf_op jit(solution)/shard_map/ppermute | solution.py:65
  171.4 15.2 %all-to-all-start.4 = ((bf16[8,8,2048]{2,1,0:T(8,128)(2,1)}), bf16[8,8,2048]{2,1,0:T(8,128)(2,1)S(1)}, u32[]{:S(2)}, u32[]{:S(2)}) async-start(bf16[8,8,2048]{2,1,0:T(8,128)(2,1)} %fusion.28), calls=%async_computation.4 | async-start | bytes 524288 | tf_op jit(solution)/shard_map/all_to_all | solution.py:60
  174.8 14.2 %collective-permute-start.24 = (f32[4,2048]{1,0:T(4,128)S(1)}, f32[4,2048]{1,0:T(4,128)S(1)}, u32[]{:S(2)}, u32[]{:S(2)}) collective-permute-start(f32[4,2048]{1,0:T(4,128)S(1)} %get-tuple-element.28), channel_id=1, source_target_pairs={{0,1},{1,0},{2,3},{3,2},{4,5},{5,4},{6,7},{7,6},{8,9},{9,8},{10,11... | collective-permute-start | bytes 98312 | tf_op jit(solution)/shard_map/ppermute | solution.py:29
  186.6 2.4 %collective-permute-start.29 = (f32[4,2048]{1,0:T(4,128)S(1)}, f32[4,2048]{1,0:T(4,128)S(1)}, u32[]{:S(2)}, u32[]{:S(2)}) collective-permute-start(f32[4,2048]{1,0:T(4,128)S(1)} %get-tuple-element.26), channel_id=1, source_target_pairs={{0,1},{1,0},{2,3},{3,2},{4,5},{5,4},{6,7},{7,6},{8,9},{9,8},{10,11... | collective-permute-start | bytes 98312 | tf_op jit(solution)/shard_map/ppermute | solution.py:29
  (11 other events, 161.0 us)

commit v4 on v3

--- a/solution.py
+++ b/solution.py
@@ -112,12 +112,22 @@
     core = lax.axis_index("c")
     n_dp = lax.axis_size("dp")
     n_mp = lax.axis_size(MP)
-    own_rows = residual.astype(F32)
-    normed_in = (own_rows * rms_scale(own_rows) * ffn_gain).astype(BF)
+    got = swap(residual)
+    half = residual.shape[1] // 2
+
+    def chip_order(a, b):
+        return jnp.where(core == 0, jnp.concatenate([a, b], 0), jnp.concatenate([b, a], 0))
+
+    def columns(x):
+        return jnp.where(core == 0, x[..., :half], x[..., half:])
+
+    scale_in = chip_order(rms_scale(residual.astype(F32)), rms_scale(got.astype(F32)))
+    block = chip_order(columns(residual), columns(got))
+    normed_in = (block.astype(F32) * scale_in * columns(ffn_gain)).astype(BF)
     member, valid = pool_masks(passage_ids[0], valid_counts[0])
     member, valid = local_rows(member), local_rows(valid)
     gate_up = jnp.concatenate([gate_weight, up_weight], axis=1)
-    mine, theirs = gather(chip_rows(normed_in, core))
+    mine, theirs = gather(normed_in)
     residual8 = chip_rows(residual, core).astype(F32)
     gain8 = halves(final_gain[None, :], core, 1)[0]
 
@@ -136,7 +146,7 @@
     scale = rms_scale(hidden)
 
     head_own, head_other = lax.optimization_barrier(halves(head_weight, core, 0))
-    logits = both_halves(mine, theirs, head_own, head_other)
+    logits = lax.optimization_barrier(both_halves(mine, theirs, head_own, head_other))
     positive = jnp.maximum(logits, 0.0)
     weights = jnp.log1p(positive)
     powered = valid[:, None] * weights**4
@@ -151,9 +161,8 @@
     log_smooth = jnp.log(smooth)
     sums = jnp.stack([jnp.sum(smooth, axis=0), jnp.sum(smooth * log_smooth, axis=0)])
     sums = exchange(jnp.broadcast_to(sums[None], (n_mp, 2, 128)), MP)
-    slope = lax.optimization_barrier(valid[:, None] * weights**3 / (1.0 + positive))
     row_factor = jnp.dot(member, (1.0 + pooled_sum) ** (-0.75), precision=highest)
-    slope = lax.optimization_barrier(slope * row_factor)
+    slope = lax.optimization_barrier(valid[:, None] * weights**3 * row_factor / (1.0 + positive))
     sums = jnp.sum(jnp.sum(sums, axis=0), axis=1)
     total, spread = sums[0], sums[1]
     entropy = jnp.log(total) - spread / total

time: 192 us -> 193 us (level)
  starting transfers between devices: 60.8 us -> 54.6 us
  waiting for transfers between devices: 90.6 us -> 96.7 us
    ppermute x12, waiting for transfers between devices: 41 us -> 47.2 us  [along_y(): return lax.ppermute(x, 'y', [(i, (i + k) % n) for i in range(n)])]
    ppermute x15, starting transfers between devices: 19.7 us -> 13.5 us  [swap(): return lax.ppermute(x, 'c', [(0, 1), (1, 0)])]
    dynamic_slice x4 -> x3, local copies, waits for them, and re-layouts: 7.79 us -> 7.74 us  [halves(): other = lax.dynamic_slice_in_dim(x, (1 - core) * size, size, axis)]
  transfers between devices with their start and end apart: 35 -> 35, of which waited for: 22 -> 21; matrix products, arithmetic and copies ran while one was open for 10% -> 12% of each run, Pallas kernels for 0% -> 0%
where the time goes in v4:
time: 193 us; the launch traced here: 192 us
  waiting for transfers between devices  96.7 us (50%)
  starting transfers between devices  54.6 us (28%)
  local copies, waits for them, and re-layouts  14.3 us (7%)
  matrix products  14.2 us (7%)
  other arithmetic  7.84 us (4%)
  between operations  4.26 us (2%)
    ppermute x12, waiting for transfers between devices, along_y(): return lax.ppermute(x, 'y', [(i, (i + k) % n) for i in range(n)])  47.2 us
    all_to_all x5, waiting for transfers between devices, exchange(): return lax.all_to_all(x, axes, 0, 0)  41.4 us
    all_to_all x5, starting transfers between devices, exchange(): return lax.all_to_all(x, axes, 0, 0)  26.5 us
    ppermute x15, starting transfers between devices, swap(): return lax.ppermute(x, 'c', [(0, 1), (1, 0)])  13.5 us
    ppermute x12, starting transfers between devices, along_y(): return lax.ppermute(x, 'y', [(i, (i + k) % n) for i in range(n)])  11.6 us
    dynamic_slice x3, local copies, waits for them, and re-layouts, halves(): other = lax.dynamic_slice_in_dim(x, (1 - core) * size, size, axis)  7.74 us
    dot_general x6, matrix products, mm(): return jnp.dot(a, b, preferred_element_type=F32)  6.66 us
    dot_general x2, matrix products, mm_t(): lax.dot_general(a, b, (((1,), (1,)), ((), ())), preferred_element_type=F32)  4.97 us
  transfers between devices with their start and end apart: 35, of which 21 were waited for; matrix products, arithmetic and copies ran while one was open for 12% of the time, Pallas kernels for 0%

profile of v4, /device:TPU:31, one launch (start us, length us, event | category | flops | bytes accessed | tf_op | source)
XLA Modules:
  0.0 191.9 jit_solution(2371733891640950951)
XLA Ops:
  4.9 8.2 %all-to-all-start = ((bf16[8,8,2048]{2,1,0:T(8,128)(2,1)}), bf16[8,8,2048]{2,1,0:T(8,128)(2,1)S(1)}, u32[]{:S(2)}, u32[]{:S(2)}) async-start(bf16[8,8,2048]{2,1,0:T(8,128)(2,1)} %broadcast_in_dim.56), calls=%async_computation | async-start | bytes 524288 | tf_op jit(solution)/shard_map/all_to_all | solution.py:60
  14.5 10.9 %all-to-all-done = bf16[8,8,2048]{2,1,0:T(8,128)(2,1)S(1)} async-done(((bf16[8,8,2048]{2,1,0:T(8,128)(2,1)}), bf16[8,8,2048]{2,1,0:T(8,128)(2,1)S(1)}, u32[]{:S(2)}, u32[]{:S(2)}) %all-to-all-start) | async-done | bytes 262176 | tf_op jit(solution)/shard_map/all_to_all | solution.py:60
  26.6 1.9 collective-permute-start.4
  28.5 1.5 constant_dynamic-update-slice_fusion
  29.9 1.4 collective-permute-start.5
  31.4 8.2 %collective-permute-done.2 = bf16[64,2048]{1,0:T(8,128)(2,1)S(1)} collective-permute-done((bf16[64,2048]{1,0:T(8,128)(2,1)S(1)}, bf16[64,2048]{1,0:T(8,128)(2,1)S(1)}, u32[]{:S(2)}, u32[]{:S(2)}) %collective-permute-start.2) | collective-permute-done | bytes 262176 | tf_op jit(solution)/shard_map/ppermute | solution.py:65
  44.9 1.9 collective-permute-done.9
  46.9 2.3 %collective-permute-start.10 = (bf16[64,2048]{1,0:T(8,128)(2,1)S(1)}, bf16[64,2048]{1,0:T(8,128)(2,1)S(1)}, u32[]{:S(2)}, u32[]{:S(2)}) collective-permute-start(bf16[64,2048]{1,0:T(8,128)(2,1)S(1)} %get-tuple-element.23), channel_id=1, source_target_pairs={{0,2},{2,4},{4,6},{6,0},{1,3},{3,5},{5,7},{7,1},{8,10},{10,12},{12... | collective-permute-start | bytes 786440 | tf_op jit(solution)/shard_map/ppermute | solution.py:65
  49.9 5.1 %collective-permute-done.10 = bf16[64,2048]{1,0:T(8,128)(2,1)S(1)} collective-permute-done((bf16[64,2048]{1,0:T(8,128)(2,1)S(1)}, bf16[64,2048]{1,0:T(8,128)(2,1)S(1)}, u32[]{:S(2)}, u32[]{:S(2)}) %collective-permute-start.10) | collective-permute-done | bytes 262176 | tf_op jit(solution)/shard_map/ppermute | solution.py:65
  55.0 3.0 %collective-permute-done.11 = bf16[64,2048]{1,0:T(8,128)(2,1)S(1)} collective-permute-done((bf16[64,2048]{1,0:T(8,128)(2,1)S(1)}, bf16[64,2048]{1,0:T(8,128)(2,1)S(1)}, u32[]{:S(2)}, u32[]{:S(2)}) %collective-permute-start.11) | collective-permute-done | bytes 262176 | tf_op jit(solution)/shard_map/ppermute | solution.py:65
  58.0 6.0 %collective-permute-done.12 = bf16[64,2048]{1,0:T(8,128)(2,1)S(1)} collective-permute-done((bf16[64,2048]{1,0:T(8,128)(2,1)S(1)}, bf16[64,2048]{1,0:T(8,128)(2,1)S(1)}, u32[]{:S(2)}, u32[]{:S(2)}) %collective-permute-start.12) | collective-permute-done | bytes 262176 | tf_op jit(solution)/shard_map/ppermute | solution.py:65
  64.8 3.4 %all-to-all-start.1 = ((bf16[8,8,2048]{2,1,0:T(8,128)(2,1)}), bf16[8,8,2048]{2,1,0:T(8,128)(2,1)S(1)}, u32[]{:S(2)}, u32[]{:S(2)}) async-start(bf16[8,8,2048]{2,1,0:T(8,128)(2,1)} %fusion.28), calls=%async_computation.1 | async-start | bytes 524288 | tf_op jit(solution)/shard_map/all_to_all | solution.py:60
  69.3 7.7 %constant_dynamic-slice_fusion.4 = (bf16[2048,1024]{1,0:T(8,128)(2,1)}, bf16[2048,1024]{1,0:T(8,128)(2,1)}) fusion(bf16[4096,1024]{1,0:T(8,128)(2,1)} %param.15, s32[]{:T(128)S(6)} %select_n.102, s32[]{:T(128)} %select_n.101), kind=kLoop, calls=%fused_computation.100 | loop fusion | bytes 16777224 | tf_op jit(solution)/shard_map/dynamic_slice | solution.py:43
  77.0 1.9 all-to-all-done.1
  79.1 2.1 %collective-permute-start.13 = (f32[8,1]{0,1:T(1,128)S(1)}, f32[8,1]{0,1:T(1,128)S(1)}, u32[]{:S(2)}, u32[]{:S(2)}) collective-permute-start(f32[8,1]{0,1:T(1,128)S(1)} %bitcast.60), channel_id=1, source_target_pairs={{0,1},{1,0},{2,3},{3,2},{4,5},{5,4},{6,7},{7,6},{8,9},{9,8},{10,11... | collective-permute-start | bytes 104 | tf_op jit(solution)/shard_map/ppermute | solution.py:29
  82.9 3.4 %all-to-all-start.2 = ((bf16[8,8,2048]{2,1,0:T(8,128)(2,1)}), bf16[8,8,2048]{2,1,0:T(8,128)(2,1)S(1)}, u32[]{:S(2)}, u32[]{:S(2)}) async-start(bf16[8,8,2048]{2,1,0:T(8,128)(2,1)} %broadcast_in_dim.58), calls=%async_computation.2 | async-start | bytes 524288 | tf_op jit(solution)/shard_map/all_to_all | solution.py:60
  88.2 10.4 %all-to-all-done.2 = bf16[8,8,2048]{2,1,0:T(8,128)(2,1)S(1)} async-done(((bf16[8,8,2048]{2,1,0:T(8,128)(2,1)}), bf16[8,8,2048]{2,1,0:T(8,128)(2,1)S(1)}, u32[]{:S(2)}, u32[]{:S(2)}) %all-to-all-start.2) | async-done | bytes 262176 | tf_op jit(solution)/shard_map/all_to_all | solution.py:60
  102.8 10.0 %collective-permute-done.14 = bf16[64,2048]{1,0:T(8,128)(2,1)S(1)} collective-permute-done((bf16[64,2048]{1,0:T(8,128)(2,1)S(1)}, bf16[64,2048]{1,0:T(8,128)(2,1)S(1)}, u32[]{:S(2)}, u32[]{:S(2)}) %collective-permute-start.14) | collective-permute-done | bytes 262176 | tf_op jit(solution)/shard_map/ppermute | solution.py:65
  113.3 1.7 collective-permute-start.18
  115.5 3.6 %fusion.48 = f32[256,1024]{1,0:T(8,128)S(1)} fusion(bf16[256,2048]{1,0:T(8,128)(2,1)S(1)} %pad_maximum_fusion.2, bf16[2048,1024]{1,0:T(8,128)(2,1)} %get-tuple-element.5), kind=kOutput, calls=%fused_computation.121 | convolution fusion | flops 1073741824 | bytes 6291456 | tf_op jit(solution)/shard_map/dot_general | solution.py:33
  120.6 1.5 fusion.46
  123.2 1.8 collective-permute-start.22
  126.0 2.6 %collective-permute-done.23 = f32[8,128]{1,0:T(8,128)S(1)} collective-permute-done((f32[8,128]{1,0:T(8,128)S(1)}, f32[8,128]{1,0:T(8,128)S(1)}, u32[]{:S(2)}, u32[]{:S(2)}) %collective-permute-start.23) | collective-permute-done | bytes 4128 | tf_op jit(solution)/shard_map/ppermute | solution.py:157
  129.4 8.1 %all-to-all-start.3 = ((f32[64,2,128]{2,1,0:T(2,128)}), f32[64,2,128]{2,1,0:T(2,128)S(1)}, u32[]{:S(2)}, u32[]{:S(2)}) async-start(f32[64,2,128]{2,1,0:T(2,128)} %broadcast_in_dim.59), calls=%async_computation.3 | async-start | bytes 131072 | tf_op jit(solution)/shard_map/all_to_all | solution.py:60
  138.5 7.0 %all-to-all-done.3 = f32[64,2,128]{2,1,0:T(2,128)S(1)} async-done(((f32[64,2,128]{2,1,0:T(2,128)}), f32[64,2,128]{2,1,0:T(2,128)S(1)}, u32[]{:S(2)}, u32[]{:S(2)}) %all-to-all-start.3) | async-done | bytes 65568 | tf_op jit(solution)/shard_map/all_to_all | solution.py:60
  147.2 3.7 %convolution_convert_fusion.1 = bf16[256,2048]{1,0:T(8,128)(2,1)S(1)} fusion(bf16[256,1024]{1,0:T(8,128)(2,1)S(1)} %multiply_convert_fusion, bf16[2048,1024]{1,0:T(8,128)(2,1)} %get-tuple-element.6), kind=kOutput, calls=%fused_computation.1 | convolution fusion | flops 1074266112 | bytes 5767168 | tf_op jit(solution)/shard_map/dot_general | solution.py:37
  153.8 2.1 %collective-permute-start.26 = (bf16[64,2048]{1,0:T(8,128)(2,1)S(1)}, bf16[64,2048]{1,0:T(8,128)(2,1)S(1)}, u32[]{:S(2)}, u32[]{:S(2)}) collective-permute-start(bf16[64,2048]{1,0:T(8,128)(2,1)S(1)} %get-tuple-element.20), channel_id=1, source_target_pairs={{0,2},{2,4},{4,6},{6,0},{1,3},{3,5},{5,7},{7,1},{8,10},{10,12},{12... | collective-permute-start | bytes 786440 | tf_op jit(solution)/shard_map/ppermute | solution.py:65
  156.8 4.8 %collective-permute-done.26 = bf16[64,2048]{1,0:T(8,128)(2,1)S(1)} collective-permute-done((bf16[64,2048]{1,0:T(8,128)(2,1)S(1)}, bf16[64,2048]{1,0:T(8,128)(2,1)S(1)}, u32[]{:S(2)}, u32[]{:S(2)}) %collective-permute-start.26) | collective-permute-done | bytes 262176 | tf_op jit(solution)/shard_map/ppermute | solution.py:65
  161.6 3.1 %collective-permute-done.27 = bf16[64,2048]{1,0:T(8,128)(2,1)S(1)} collective-permute-done((bf16[64,2048]{1,0:T(8,128)(2,1)S(1)}, bf16[64,2048]{1,0:T(8,128)(2,1)S(1)}, u32[]{:S(2)}, u32[]{:S(2)}) %collective-permute-start.27) | collective-permute-done | bytes 262176 | tf_op jit(solution)/shard_map/ppermute | solution.py:65
  164.7 6.6 %collective-permute-done.28 = bf16[64,2048]{1,0:T(8,128)(2,1)S(1)} collective-permute-done((bf16[64,2048]{1,0:T(8,128)(2,1)S(1)}, bf16[64,2048]{1,0:T(8,128)(2,1)S(1)}, u32[]{:S(2)}, u32[]{:S(2)}) %collective-permute-start.28) | collective-permute-done | bytes 262176 | tf_op jit(solution)/shard_map/ppermute | solution.py:65
  172.1 3.4 %all-to-all-start.4 = ((bf16[8,8,2048]{2,1,0:T(8,128)(2,1)}), bf16[8,8,2048]{2,1,0:T(8,128)(2,1)S(1)}, u32[]{:S(2)}, u32[]{:S(2)}) async-start(bf16[8,8,2048]{2,1,0:T(8,128)(2,1)} %fusion.29), calls=%async_computation.4 | async-start | bytes 524288 | tf_op jit(solution)/shard_map/all_to_all | solution.py:60
  176.2 11.2 %all-to-all-done.4 = bf16[8,8,2048]{2,1,0:T(8,128)(2,1)S(1)} async-done(((bf16[8,8,2048]{2,1,0:T(8,128)(2,1)}), bf16[8,8,2048]{2,1,0:T(8,128)(2,1)S(1)}, u32[]{:S(2)}, u32[]{:S(2)}) %all-to-all-start.4) | async-done | bytes 262176 | tf_op jit(solution)/shard_map/all_to_all | solution.py:60
  (117 shorter events, 37.1 us)
Async XLA Ops:
  0.6 3.2 %collective-permute-start.1 = (bf16[4,4096]{1,0:T(4,128)(2,1)}, bf16[4,4096]{1,0:T(4,128)(2,1)S(1)}, u32[]{:S(2)}, u32[]{:S(2)}) collective-permute-start(bf16[4,4096]{1,0:T(4,128)(2,1)} %param.9), channel_id=1, source_target_pairs={{0,1},{1,0},{2,3},{3,2},{4,5},{5,4},{6,7},{7,6},{8,9},{9,8},{10,11... | collective-permute-start | bytes 98312 | tf_op jit(solution)/shard_map/ppermute | solution.py:29
  4.9 20.5 %all-to-all-start = ((bf16[8,8,2048]{2,1,0:T(8,128)(2,1)}), bf16[8,8,2048]{2,1,0:T(8,128)(2,1)S(1)}, u32[]{:S(2)}, u32[]{:S(2)}) async-start(bf16[8,8,2048]{2,1,0:T(8,128)(2,1)} %broadcast_in_dim.56), calls=%async_computation | async-start | bytes 524288 | tf_op jit(solution)/shard_map/all_to_all | solution.py:60
  25.4 14.2 %collective-permute-start.2 = (bf16[64,2048]{1,0:T(8,128)(2,1)S(1)}, bf16[64,2048]{1,0:T(8,128)(2,1)S(1)}, u32[]{:S(2)}, u32[]{:S(2)}) collective-permute-start(bf16[64,2048]{1,0:T(8,128)(2,1)S(1)} %bitcast.48), channel_id=1, source_target_pairs={{0,6},{2,0},{4,2},{6,4},{1,7},{3,1},{5,3},{7,5},{8,14},{10,8},{12,... | collective-permute-start | bytes 786440 | tf_op jit(solution)/shard_map/ppermute | solution.py:65
  25.9 15.1 %collective-permute-start.3 = (bf16[64,2048]{1,0:T(8,128)(2,1)S(1)}, bf16[64,2048]{1,0:T(8,128)(2,1)S(1)}, u32[]{:S(2)}, u32[]{:S(2)}) collective-permute-start(bf16[64,2048]{1,0:T(8,128)(2,1)S(1)} %bitcast.49), channel_id=1, source_target_pairs={{0,4},{2,6},{4,0},{6,2},{1,5},{3,7},{5,1},{7,3},{8,12},{10,14},{12... | collective-permute-start | bytes 786440 | tf_op jit(solution)/shard_map/ppermute | solution.py:65
  26.6 14.4 %collective-permute-start.4 = (bf16[64,2048]{1,0:T(8,128)(2,1)S(1)}, bf16[64,2048]{1,0:T(8,128)(2,1)S(1)}, u32[]{:S(2)}, u32[]{:S(2)}) collective-permute-start(bf16[64,2048]{1,0:T(8,128)(2,1)S(1)} %bitcast.50), channel_id=1, source_target_pairs={{0,2},{2,4},{4,6},{6,0},{1,3},{3,5},{5,7},{7,1},{8,10},{10,12},{12... | collective-permute-start | bytes 786440 | tf_op jit(solution)/shard_map/ppermute | solution.py:65
  29.9 12.2 %collective-permute-start.5 = (bf16[64,2048]{1,0:T(8,128)(2,1)S(1)}, bf16[64,2048]{1,0:T(8,128)(2,1)S(1)}, u32[]{:S(2)}, u32[]{:S(2)}) collective-permute-start(bf16[64,2048]{1,0:T(8,128)(2,1)S(1)} %bitcast.51), channel_id=1, source_target_pairs={{0,1},{1,0},{2,3},{3,2},{4,5},{5,4},{6,7},{7,6},{8,9},{9,8},{10,11... | collective-permute-start | bytes 786440 | tf_op jit(solution)/shard_map/ppermute | solution.py:29
  39.6 2.6 %collective-permute-start.6 = (bf16[64,2048]{1,0:T(8,128)(2,1)S(1)}, bf16[64,2048]{1,0:T(8,128)(2,1)S(1)}, u32[]{:S(2)}, u32[]{:S(2)}) collective-permute-start(bf16[64,2048]{1,0:T(8,128)(2,1)S(1)} %collective-permute-done.2), channel_id=1, source_target_pairs={{0,1},{1,0},{2,3},{3,2},{4,5},{5,4},{6,7},{7,6},{8,9},{9,8},{10,11... | collective-permute-start | bytes 786440 | tf_op jit(solution)/shard_map/ppermute | solution.py:29
  44.0 2.7 %collective-permute-start.9 = (bf16[256,2048]{1,0:T(8,128)(2,1)S(1)}, bf16[256,2048]{1,0:T(8,128)(2,1)S(1)}, u32[]{:S(2)}, u32[]{:S(2)}) collective-permute-start(bf16[256,2048]{1,0:T(8,128)(2,1)S(1)} %convolution_convert_fusion), channel_id=1, source_target_pairs={{0,1},{1,0},{2,3},{3,2},{4,5},{5,4},{6,7},{7,6},{8,9},{9,8},{10,11... | collective-permute-start | bytes 3145736 | tf_op jit(solution)/shard_map/ppermute | solution.py:29
  46.9 8.1 %collective-permute-start.10 = (bf16[64,2048]{1,0:T(8,128)(2,1)S(1)}, bf16[64,2048]{1,0:T(8,128)(2,1)S(1)}, u32[]{:S(2)}, u32[]{:S(2)}) collective-permute-start(bf16[64,2048]{1,0:T(8,128)(2,1)S(1)} %get-tuple-element.23), channel_id=1, source_target_pairs={{0,2},{2,4},{4,6},{6,0},{1,3},{3,5},{5,7},{7,1},{8,10},{10,12},{12... | collective-permute-start | bytes 786440 | tf_op jit(solution)/shard_map/ppermute | solution.py:65
  49.2 8.8 %collective-permute-start.11 = (bf16[64,2048]{1,0:T(8,128)(2,1)S(1)}, bf16[64,2048]{1,0:T(8,128)(2,1)S(1)}, u32[]{:S(2)}, u32[]{:S(2)}) collective-permute-start(bf16[64,2048]{1,0:T(8,128)(2,1)S(1)} %get-tuple-element.25), channel_id=1, source_target_pairs={{0,4},{2,6},{4,0},{6,2},{1,5},{3,7},{5,1},{7,3},{8,12},{10,14},{12... | collective-permute-start | bytes 786440 | tf_op jit(solution)/shard_map/ppermute | solution.py:65
  49.2 14.8 %collective-permute-start.12 = (bf16[64,2048]{1,0:T(8,128)(2,1)S(1)}, bf16[64,2048]{1,0:T(8,128)(2,1)S(1)}, u32[]{:S(2)}, u32[]{:S(2)}) collective-permute-start(bf16[64,2048]{1,0:T(8,128)(2,1)S(1)} %get-tuple-element.24), channel_id=1, source_target_pairs={{0,6},{2,0},{4,2},{6,4},{1,7},{3,1},{5,3},{7,5},{8,14},{10,8},{12,... | collective-permute-start | bytes 786440 | tf_op jit(solution)/shard_map/ppermute | solution.py:65
  64.8 14.1 %all-to-all-start.1 = ((bf16[8,8,2048]{2,1,0:T(8,128)(2,1)}), bf16[8,8,2048]{2,1,0:T(8,128)(2,1)S(1)}, u32[]{:S(2)}, u32[]{:S(2)}) async-start(bf16[8,8,2048]{2,1,0:T(8,128)(2,1)} %fusion.28), calls=%async_computation.1 | async-start | bytes 524288 | tf_op jit(solution)/shard_map/all_to_all | solution.py:60
  68.3 10.7 %collective-permute-start = (bf16[4,2048]{1,0:T(4,128)(2,1)S(1)}, bf16[4,2048]{1,0:T(4,128)(2,1)S(1)}, u32[]{:S(2)}, u32[]{:S(2)}) collective-permute-start(bf16[4,2048]{1,0:T(4,128)(2,1)S(1)} %get-tuple-element.30), channel_id=1, source_target_pairs={{0,1},{1,0},{2,3},{3,2},{4,5},{5,4},{6,7},{7,6},{8,9},{9,8},{10,11... | collective-permute-start | bytes 49160 | tf_op jit(solution)/shard_map/ppermute | solution.py:29
  79.1 3.0 %collective-permute-start.13 = (f32[8,1]{0,1:T(1,128)S(1)}, f32[8,1]{0,1:T(1,128)S(1)}, u32[]{:S(2)}, u32[]{:S(2)}) collective-permute-start(f32[8,1]{0,1:T(1,128)S(1)} %bitcast.60), channel_id=1, source_target_pairs={{0,1},{1,0},{2,3},{3,2},{4,5},{5,4},{6,7},{7,6},{8,9},{9,8},{10,11... | collective-permute-start | bytes 104 | tf_op jit(solution)/shard_map/ppermute | solution.py:29
  82.9 15.7 %all-to-all-start.2 = ((bf16[8,8,2048]{2,1,0:T(8,128)(2,1)}), bf16[8,8,2048]{2,1,0:T(8,128)(2,1)S(1)}, u32[]{:S(2)}, u32[]{:S(2)}) async-start(bf16[8,8,2048]{2,1,0:T(8,128)(2,1)} %broadcast_in_dim.58), calls=%async_computation.2 | async-start | bytes 524288 | tf_op jit(solution)/shard_map/all_to_all | solution.py:60
  98.6 14.2 %collective-permute-start.14 = (bf16[64,2048]{1,0:T(8,128)(2,1)S(1)}, bf16[64,2048]{1,0:T(8,128)(2,1)S(1)}, u32[]{:S(2)}, u32[]{:S(2)}) collective-permute-start(bf16[64,2048]{1,0:T(8,128)(2,1)S(1)} %bitcast.43), channel_id=1, source_target_pairs={{0,6},{2,0},{4,2},{6,4},{1,7},{3,1},{5,3},{7,5},{8,14},{10,8},{12,... | collective-permute-start | bytes 786440 | tf_op jit(solution)/shard_map/ppermute | solution.py:65
  98.6 14.2 %collective-permute-start.15 = (bf16[64,2048]{1,0:T(8,128)(2,1)S(1)}, bf16[64,2048]{1,0:T(8,128)(2,1)S(1)}, u32[]{:S(2)}, u32[]{:S(2)}) collective-permute-start(bf16[64,2048]{1,0:T(8,128)(2,1)S(1)} %bitcast.44), channel_id=1, source_target_pairs={{0,4},{2,6},{4,0},{6,2},{1,5},{3,7},{5,1},{7,3},{8,12},{10,14},{12... | collective-permute-start | bytes 786440 | tf_op jit(solution)/shard_map/ppermute | solution.py:65
  99.9 13.3 %collective-permute-start.16 = (bf16[64,2048]{1,0:T(8,128)(2,1)S(1)}, bf16[64,2048]{1,0:T(8,128)(2,1)S(1)}, u32[]{:S(2)}, u32[]{:S(2)}) collective-permute-start(bf16[64,2048]{1,0:T(8,128)(2,1)S(1)} %bitcast.45), channel_id=1, source_target_pairs={{0,2},{2,4},{4,6},{6,0},{1,3},{3,5},{5,7},{7,1},{8,10},{10,12},{12... | collective-permute-start | bytes 786440 | tf_op jit(solution)/shard_map/ppermute | solution.py:65
  101.5 17.6 %collective-permute-start.17 = (bf16[64,2048]{1,0:T(8,128)(2,1)S(1)}, bf16[64,2048]{1,0:T(8,128)(2,1)S(1)}, u32[]{:S(2)}, u32[]{:S(2)}) collective-permute-start(bf16[64,2048]{1,0:T(8,128)(2,1)S(1)} %bitcast.46), channel_id=1, source_target_pairs={{0,1},{1,0},{2,3},{3,2},{4,5},{5,4},{6,7},{7,6},{8,9},{9,8},{10,11... | collective-permute-start | bytes 786440 | tf_op jit(solution)/shard_map/ppermute | solution.py:29
  113.3 5.8 %collective-permute-start.18 = (bf16[64,2048]{1,0:T(8,128)(2,1)S(1)}, bf16[64,2048]{1,0:T(8,128)(2,1)S(1)}, u32[]{:S(2)}, u32[]{:S(2)}) collective-permute-start(bf16[64,2048]{1,0:T(8,128)(2,1)S(1)} %collective-permute-done.14), channel_id=1, source_target_pairs={{0,1},{1,0},{2,3},{3,2},{4,5},{5,4},{6,7},{7,6},{8,9},{9,8},{10,11... | collective-permute-start | bytes 786440 | tf_op jit(solution)/shard_map/ppermute | solution.py:29
  115.0 4.2 %collective-permute-start.19 = (bf16[64,2048]{1,0:T(8,128)(2,1)S(1)}, bf16[64,2048]{1,0:T(8,128)(2,1)S(1)}, u32[]{:S(2)}, u32[]{:S(2)}) collective-permute-start(bf16[64,2048]{1,0:T(8,128)(2,1)S(1)} %collective-permute-done.15), channel_id=1, source_target_pairs={{0,1},{1,0},{2,3},{3,2},{4,5},{5,4},{6,7},{7,6},{8,9},{9,8},{10,11... | collective-permute-start | bytes 786440 | tf_op jit(solution)/shard_map/ppermute | solution.py:29
  115.1 4.1 %collective-permute-start.20 = (bf16[64,2048]{1,0:T(8,128)(2,1)S(1)}, bf16[64,2048]{1,0:T(8,128)(2,1)S(1)}, u32[]{:S(2)}, u32[]{:S(2)}) collective-permute-start(bf16[64,2048]{1,0:T(8,128)(2,1)S(1)} %collective-permute-done.16), channel_id=1, source_target_pairs={{0,1},{1,0},{2,3},{3,2},{4,5},{5,4},{6,7},{7,6},{8,9},{9,8},{10,11... | collective-permute-start | bytes 786440 | tf_op jit(solution)/shard_map/ppermute | solution.py:29
  122.1 4.0 %collective-permute-start.21 = (f32[8,128]{1,0:T(8,128)S(1)}, f32[8,128]{1,0:T(8,128)S(1)}, u32[]{:S(2)}, u32[]{:S(2)}) collective-permute-start(f32[8,128]{1,0:T(8,128)S(1)} %bitcast.55), channel_id=1, source_target_pairs={{0,128},{64,192},{128,0},{192,64},{1,129},{65,193},{129,1},{193,65... | collective-permute-start | bytes 12296 | tf_op jit(solution)/shard_map/ppermute | solution.py:157
  123.2 2.8 %collective-permute-start.22 = (f32[8,128]{1,0:T(8,128)S(1)}, f32[8,128]{1,0:T(8,128)S(1)}, u32[]{:S(2)}, u32[]{:S(2)}) collective-permute-start(f32[8,128]{1,0:T(8,128)S(1)} %bitcast.56), channel_id=1, source_target_pairs={{0,64},{64,128},{128,192},{192,0},{1,65},{65,129},{129,193},{193,1... | collective-permute-start | bytes 12296 | tf_op jit(solution)/shard_map/ppermute | solution.py:157
  125.0 3.7 %collective-permute-start.23 = (f32[8,128]{1,0:T(8,128)S(1)}, f32[8,128]{1,0:T(8,128)S(1)}, u32[]{:S(2)}, u32[]{:S(2)}) collective-permute-start(f32[8,128]{1,0:T(8,128)S(1)} %bitcast.57), channel_id=1, source_target_pairs={{0,192},{64,0},{128,64},{192,128},{1,193},{65,1},{129,65},{193,129... | collective-permute-start | bytes 12296 | tf_op jit(solution)/shard_map/ppermute | solution.py:157
  129.4 16.2 %all-to-all-start.3 = ((f32[64,2,128]{2,1,0:T(2,128)}), f32[64,2,128]{2,1,0:T(2,128)S(1)}, u32[]{:S(2)}, u32[]{:S(2)}) async-start(f32[64,2,128]{2,1,0:T(2,128)} %broadcast_in_dim.59), calls=%async_computation.3 | async-start | bytes 131072 | tf_op jit(solution)/shard_map/all_to_all | solution.py:60
  150.8 2.8 %collective-permute-start.25 = (bf16[256,2048]{1,0:T(8,128)(2,1)S(1)}, bf16[256,2048]{1,0:T(8,128)(2,1)S(1)}, u32[]{:S(2)}, u32[]{:S(2)}) collective-permute-start(bf16[256,2048]{1,0:T(8,128)(2,1)S(1)} %convolution_convert_fusion.1), channel_id=1, source_target_pairs={{0,1},{1,0},{2,3},{3,2},{4,5},{5,4},{6,7},{7,6},{8,9},{9,8},{10,11... | collective-permute-start | bytes 3145736 | tf_op jit(solution)/shard_map/ppermute | solution.py:29
  153.8 7.8 %collective-permute-start.26 = (bf16[64,2048]{1,0:T(8,128)(2,1)S(1)}, bf16[64,2048]{1,0:T(8,128)(2,1)S(1)}, u32[]{:S(2)}, u32[]{:S(2)}) collective-permute-start(bf16[64,2048]{1,0:T(8,128)(2,1)S(1)} %get-tuple-element.20), channel_id=1, source_target_pairs={{0,2},{2,4},{4,6},{6,0},{1,3},{3,5},{5,7},{7,1},{8,10},{10,12},{12... | collective-permute-start | bytes 786440 | tf_op jit(solution)/shard_map/ppermute | solution.py:65
  155.9 8.8 %collective-permute-start.27 = (bf16[64,2048]{1,0:T(8,128)(2,1)S(1)}, bf16[64,2048]{1,0:T(8,128)(2,1)S(1)}, u32[]{:S(2)}, u32[]{:S(2)}) collective-permute-start(bf16[64,2048]{1,0:T(8,128)(2,1)S(1)} %get-tuple-element.22), channel_id=1, source_target_pairs={{0,4},{2,6},{4,0},{6,2},{1,5},{3,7},{5,1},{7,3},{8,12},{10,14},{12... | collective-permute-start | bytes 786440 | tf_op jit(solution)/shard_map/ppermute | solution.py:65
  156.4 14.9 %collective-permute-start.28 = (bf16[64,2048]{1,0:T(8,128)(2,1)S(1)}, bf16[64,2048]{1,0:T(8,128)(2,1)S(1)}, u32[]{:S(2)}, u32[]{:S(2)}) collective-permute-start(bf16[64,2048]{1,0:T(8,128)(2,1)S(1)} %get-tuple-element.21), channel_id=1, source_target_pairs={{0,6},{2,0},{4,2},{6,4},{1,7},{3,1},{5,3},{7,5},{8,14},{10,8},{12,... | collective-permute-start | bytes 786440 | tf_op jit(solution)/shard_map/ppermute | solution.py:65
  172.1 15.2 %all-to-all-start.4 = ((bf16[8,8,2048]{2,1,0:T(8,128)(2,1)}), bf16[8,8,2048]{2,1,0:T(8,128)(2,1)S(1)}, u32[]{:S(2)}, u32[]{:S(2)}) async-start(bf16[8,8,2048]{2,1,0:T(8,128)(2,1)} %fusion.29), calls=%async_computation.4 | async-start | bytes 524288 | tf_op jit(solution)/shard_map/all_to_all | solution.py:60
  175.6 14.2 %collective-permute-start.24 = (f32[4,2048]{1,0:T(4,128)S(1)}, f32[4,2048]{1,0:T(4,128)S(1)}, u32[]{:S(2)}, u32[]{:S(2)}) collective-permute-start(f32[4,2048]{1,0:T(4,128)S(1)} %get-tuple-element.28), channel_id=1, source_target_pairs={{0,1},{1,0},{2,3},{3,2},{4,5},{5,4},{6,7},{7,6},{8,9},{9,8},{10,11... | collective-permute-start | bytes 98312 | tf_op jit(solution)/shard_map/ppermute | solution.py:29
  (10 other events, 139.7 us)

commit v5 on v4

--- a/solution.py
+++ b/solution.py
@@ -121,9 +121,9 @@
     def columns(x):
         return jnp.where(core == 0, x[..., :half], x[..., half:])
 
-    scale_in = chip_order(rms_scale(residual.astype(F32)), rms_scale(got.astype(F32)))
-    block = chip_order(columns(residual), columns(got))
-    normed_in = (block.astype(F32) * scale_in * columns(ffn_gain)).astype(BF)
+    scale_in = rms_scale(chip_order(residual, got).astype(F32))
+    block = chip_order(columns(residual), columns(got)).astype(F32)
+    normed_in = (block * scale_in * halves(ffn_gain[None, :], core, 1)[0]).astype(BF)
     member, valid = pool_masks(passage_ids[0], valid_counts[0])
     member, valid = local_rows(member), local_rows(valid)
     gate_up = jnp.concatenate([gate_weight, up_weight], axis=1)

time: 193 us -> 193 us (level)
  transfers between devices with their start and end apart: 35 -> 35, of which waited for: 21 -> 21; matrix products, arithmetic and copies ran while one was open for 12% -> 11% of each run, Pallas kernels for 0% -> 0%
where the time goes in v5:
time: 193 us; the launch traced here: 192 us
  waiting for transfers between devices  96.7 us (50%)
  starting transfers between devices  54.5 us (28%)
  local copies, waits for them, and re-layouts  15 us (8%)
  matrix products  14.2 us (7%)
  other arithmetic  6.99 us (4%)
  between operations  4.24 us (2%)
    ppermute x12, waiting for transfers between devices, along_y(): return lax.ppermute(x, 'y', [(i, (i + k) % n) for i in range(n)])  47.3 us
    all_to_all x5, waiting for transfers between devices, exchange(): return lax.all_to_all(x, axes, 0, 0)  41.4 us
    all_to_all x5, starting transfers between devices, exchange(): return lax.all_to_all(x, axes, 0, 0)  26.5 us
    ppermute x15, starting transfers between devices, swap(): return lax.ppermute(x, 'c', [(0, 1), (1, 0)])  13.5 us
    ppermute x12, starting transfers between devices, along_y(): return lax.ppermute(x, 'y', [(i, (i + k) % n) for i in range(n)])  11.6 us
    dynamic_slice x3, local copies, waits for them, and re-layouts, halves(): other = lax.dynamic_slice_in_dim(x, (1 - core) * size, size, axis)  7.75 us
    dot_general x6, matrix products, mm(): return jnp.dot(a, b, preferred_element_type=F32)  6.65 us
    dot_general x2, matrix products, mm_t(): lax.dot_general(a, b, (((1,), (1,)), ((), ())), preferred_element_type=F32)  4.97 us
  transfers between devices with their start and end apart: 35, of which 21 were waited for; matrix products, arithmetic and copies ran while one was open for 11% of the time, Pallas kernels for 0%

profile of v5, /device:TPU:31, one launch (start us, length us, event | category | flops | bytes accessed | tf_op | source)
XLA Modules:
  0.0 191.7 jit_solution(17042365649399960616)
XLA Ops:
  4.8 8.2 %all-to-all-start = ((bf16[8,8,2048]{2,1,0:T(8,128)(2,1)}), bf16[8,8,2048]{2,1,0:T(8,128)(2,1)S(1)}, u32[]{:S(2)}, u32[]{:S(2)}) async-start(bf16[8,8,2048]{2,1,0:T(8,128)(2,1)} %broadcast_in_dim.55), calls=%async_computation | async-start | bytes 524288 | tf_op jit(solution)/shard_map/all_to_all | solution.py:60
  14.4 10.9 %all-to-all-done = bf16[8,8,2048]{2,1,0:T(8,128)(2,1)S(1)} async-done(((bf16[8,8,2048]{2,1,0:T(8,128)(2,1)}), bf16[8,8,2048]{2,1,0:T(8,128)(2,1)S(1)}, u32[]{:S(2)}, u32[]{:S(2)}) %all-to-all-start) | async-done | bytes 262176 | tf_op jit(solution)/shard_map/all_to_all | solution.py:60
  26.4 1.9 collective-permute-start.4
  28.3 1.5 constant_dynamic-update-slice_fusion
  29.8 1.4 collective-permute-start.5
  31.2 8.3 %collective-permute-done.2 = bf16[64,2048]{1,0:T(8,128)(2,1)S(1)} collective-permute-done((bf16[64,2048]{1,0:T(8,128)(2,1)S(1)}, bf16[64,2048]{1,0:T(8,128)(2,1)S(1)}, u32[]{:S(2)}, u32[]{:S(2)}) %collective-permute-start.2) | collective-permute-done | bytes 262176 | tf_op jit(solution)/shard_map/ppermute | solution.py:65
  44.7 1.9 collective-permute-done.9
  46.8 2.3 %collective-permute-start.10 = (bf16[64,2048]{1,0:T(8,128)(2,1)S(1)}, bf16[64,2048]{1,0:T(8,128)(2,1)S(1)}, u32[]{:S(2)}, u32[]{:S(2)}) collective-permute-start(bf16[64,2048]{1,0:T(8,128)(2,1)S(1)} %get-tuple-element.23), channel_id=1, source_target_pairs={{0,2},{2,4},{4,6},{6,0},{1,3},{3,5},{5,7},{7,1},{8,10},{10,12},{12... | collective-permute-start | bytes 786440 | tf_op jit(solution)/shard_map/ppermute | solution.py:65
  49.8 5.2 %collective-permute-done.10 = bf16[64,2048]{1,0:T(8,128)(2,1)S(1)} collective-permute-done((bf16[64,2048]{1,0:T(8,128)(2,1)S(1)}, bf16[64,2048]{1,0:T(8,128)(2,1)S(1)}, u32[]{:S(2)}, u32[]{:S(2)}) %collective-permute-start.10) | collective-permute-done | bytes 262176 | tf_op jit(solution)/shard_map/ppermute | solution.py:65
  54.9 3.0 %collective-permute-done.11 = bf16[64,2048]{1,0:T(8,128)(2,1)S(1)} collective-permute-done((bf16[64,2048]{1,0:T(8,128)(2,1)S(1)}, bf16[64,2048]{1,0:T(8,128)(2,1)S(1)}, u32[]{:S(2)}, u32[]{:S(2)}) %collective-permute-start.11) | collective-permute-done | bytes 262176 | tf_op jit(solution)/shard_map/ppermute | solution.py:65
  57.9 6.0 %collective-permute-done.12 = bf16[64,2048]{1,0:T(8,128)(2,1)S(1)} collective-permute-done((bf16[64,2048]{1,0:T(8,128)(2,1)S(1)}, bf16[64,2048]{1,0:T(8,128)(2,1)S(1)}, u32[]{:S(2)}, u32[]{:S(2)}) %collective-permute-start.12) | collective-permute-done | bytes 262176 | tf_op jit(solution)/shard_map/ppermute | solution.py:65
  64.7 3.4 %all-to-all-start.1 = ((bf16[8,8,2048]{2,1,0:T(8,128)(2,1)}), bf16[8,8,2048]{2,1,0:T(8,128)(2,1)S(1)}, u32[]{:S(2)}, u32[]{:S(2)}) async-start(bf16[8,8,2048]{2,1,0:T(8,128)(2,1)} %fusion.28), calls=%async_computation.1 | async-start | bytes 524288 | tf_op jit(solution)/shard_map/all_to_all | solution.py:60
  69.2 7.7 %constant_dynamic-slice_fusion.4 = (bf16[2048,1024]{1,0:T(8,128)(2,1)}, bf16[2048,1024]{1,0:T(8,128)(2,1)}) fusion(bf16[4096,1024]{1,0:T(8,128)(2,1)} %param.15, s32[]{:T(128)S(6)} %select_n.90, s32[]{:T(128)} %select_n.89), kind=kLoop, calls=%fused_computation.99 | loop fusion | bytes 16777224 | tf_op jit(solution)/shard_map/dynamic_slice | solution.py:43
  76.9 1.9 all-to-all-done.1
  79.0 2.1 %collective-permute-start.13 = (f32[8,1]{0,1:T(1,128)S(1)}, f32[8,1]{0,1:T(1,128)S(1)}, u32[]{:S(2)}, u32[]{:S(2)}) collective-permute-start(f32[8,1]{0,1:T(1,128)S(1)} %bitcast.60), channel_id=1, source_target_pairs={{0,1},{1,0},{2,3},{3,2},{4,5},{5,4},{6,7},{7,6},{8,9},{9,8},{10,11... | collective-permute-start | bytes 104 | tf_op jit(solution)/shard_map/ppermute | solution.py:29
  82.8 3.4 %all-to-all-start.2 = ((bf16[8,8,2048]{2,1,0:T(8,128)(2,1)}), bf16[8,8,2048]{2,1,0:T(8,128)(2,1)S(1)}, u32[]{:S(2)}, u32[]{:S(2)}) async-start(bf16[8,8,2048]{2,1,0:T(8,128)(2,1)} %broadcast_in_dim.57), calls=%async_computation.2 | async-start | bytes 524288 | tf_op jit(solution)/shard_map/all_to_all | solution.py:60
  88.1 10.4 %all-to-all-done.2 = bf16[8,8,2048]{2,1,0:T(8,128)(2,1)S(1)} async-done(((bf16[8,8,2048]{2,1,0:T(8,128)(2,1)}), bf16[8,8,2048]{2,1,0:T(8,128)(2,1)S(1)}, u32[]{:S(2)}, u32[]{:S(2)}) %all-to-all-start.2) | async-done | bytes 262176 | tf_op jit(solution)/shard_map/all_to_all | solution.py:60
  102.7 10.0 %collective-permute-done.14 = bf16[64,2048]{1,0:T(8,128)(2,1)S(1)} collective-permute-done((bf16[64,2048]{1,0:T(8,128)(2,1)S(1)}, bf16[64,2048]{1,0:T(8,128)(2,1)S(1)}, u32[]{:S(2)}, u32[]{:S(2)}) %collective-permute-start.14) | collective-permute-done | bytes 262176 | tf_op jit(solution)/shard_map/ppermute | solution.py:65
  113.2 1.7 collective-permute-start.18
  115.4 3.6 %fusion.48 = f32[256,1024]{1,0:T(8,128)S(1)} fusion(bf16[256,2048]{1,0:T(8,128)(2,1)S(1)} %pad_maximum_fusion.2, bf16[2048,1024]{1,0:T(8,128)(2,1)} %get-tuple-element.5), kind=kOutput, calls=%fused_computation.118 | convolution fusion | flops 1073741824 | bytes 6291456 | tf_op jit(solution)/shard_map/dot_general | solution.py:33
  120.4 1.5 fusion.46
  123.1 1.8 collective-permute-start.22
  125.9 2.6 %collective-permute-done.23 = f32[8,128]{1,0:T(8,128)S(1)} collective-permute-done((f32[8,128]{1,0:T(8,128)S(1)}, f32[8,128]{1,0:T(8,128)S(1)}, u32[]{:S(2)}, u32[]{:S(2)}) %collective-permute-start.23) | collective-permute-done | bytes 4128 | tf_op jit(solution)/shard_map/ppermute | solution.py:157
  129.2 8.1 %all-to-all-start.3 = ((f32[64,2,128]{2,1,0:T(2,128)}), f32[64,2,128]{2,1,0:T(2,128)S(1)}, u32[]{:S(2)}, u32[]{:S(2)}) async-start(f32[64,2,128]{2,1,0:T(2,128)} %broadcast_in_dim.58), calls=%async_computation.3 | async-start | bytes 131072 | tf_op jit(solution)/shard_map/all_to_all | solution.py:60
  138.4 7.0 %all-to-all-done.3 = f32[64,2,128]{2,1,0:T(2,128)S(1)} async-done(((f32[64,2,128]{2,1,0:T(2,128)}), f32[64,2,128]{2,1,0:T(2,128)S(1)}, u32[]{:S(2)}, u32[]{:S(2)}) %all-to-all-start.3) | async-done | bytes 65568 | tf_op jit(solution)/shard_map/all_to_all | solution.py:60
  147.0 3.7 %convolution_convert_fusion.1 = bf16[256,2048]{1,0:T(8,128)(2,1)S(1)} fusion(bf16[256,1024]{1,0:T(8,128)(2,1)S(1)} %multiply_convert_fusion, bf16[2048,1024]{1,0:T(8,128)(2,1)} %get-tuple-element.6), kind=kOutput, calls=%fused_computation.1 | convolution fusion | flops 1074266112 | bytes 5767168 | tf_op jit(solution)/shard_map/dot_general | solution.py:37
  153.7 2.1 %collective-permute-start.26 = (bf16[64,2048]{1,0:T(8,128)(2,1)S(1)}, bf16[64,2048]{1,0:T(8,128)(2,1)S(1)}, u32[]{:S(2)}, u32[]{:S(2)}) collective-permute-start(bf16[64,2048]{1,0:T(8,128)(2,1)S(1)} %get-tuple-element.20), channel_id=1, source_target_pairs={{0,2},{2,4},{4,6},{6,0},{1,3},{3,5},{5,7},{7,1},{8,10},{10,12},{12... | collective-permute-start | bytes 786440 | tf_op jit(solution)/shard_map/ppermute | solution.py:65
  156.6 4.8 %collective-permute-done.26 = bf16[64,2048]{1,0:T(8,128)(2,1)S(1)} collective-permute-done((bf16[64,2048]{1,0:T(8,128)(2,1)S(1)}, bf16[64,2048]{1,0:T(8,128)(2,1)S(1)}, u32[]{:S(2)}, u32[]{:S(2)}) %collective-permute-start.26) | collective-permute-done | bytes 262176 | tf_op jit(solution)/shard_map/ppermute | solution.py:65
  161.5 3.1 %collective-permute-done.27 = bf16[64,2048]{1,0:T(8,128)(2,1)S(1)} collective-permute-done((bf16[64,2048]{1,0:T(8,128)(2,1)S(1)}, bf16[64,2048]{1,0:T(8,128)(2,1)S(1)}, u32[]{:S(2)}, u32[]{:S(2)}) %collective-permute-start.27) | collective-permute-done | bytes 262176 | tf_op jit(solution)/shard_map/ppermute | solution.py:65
  164.6 6.6 %collective-permute-done.28 = bf16[64,2048]{1,0:T(8,128)(2,1)S(1)} collective-permute-done((bf16[64,2048]{1,0:T(8,128)(2,1)S(1)}, bf16[64,2048]{1,0:T(8,128)(2,1)S(1)}, u32[]{:S(2)}, u32[]{:S(2)}) %collective-permute-start.28) | collective-permute-done | bytes 262176 | tf_op jit(solution)/shard_map/ppermute | solution.py:65
  172.0 3.4 %all-to-all-start.4 = ((bf16[8,8,2048]{2,1,0:T(8,128)(2,1)}), bf16[8,8,2048]{2,1,0:T(8,128)(2,1)S(1)}, u32[]{:S(2)}, u32[]{:S(2)}) async-start(bf16[8,8,2048]{2,1,0:T(8,128)(2,1)} %fusion.29), calls=%async_computation.4 | async-start | bytes 524288 | tf_op jit(solution)/shard_map/all_to_all | solution.py:60
  176.0 11.2 %all-to-all-done.4 = bf16[8,8,2048]{2,1,0:T(8,128)(2,1)S(1)} async-done(((bf16[8,8,2048]{2,1,0:T(8,128)(2,1)}), bf16[8,8,2048]{2,1,0:T(8,128)(2,1)S(1)}, u32[]{:S(2)}, u32[]{:S(2)}) %all-to-all-start.4) | async-done | bytes 262176 | tf_op jit(solution)/shard_map/all_to_all | solution.py:60
  (114 shorter events, 36.9 us)
Async XLA Ops:
  4.8 20.5 %all-to-all-start = ((bf16[8,8,2048]{2,1,0:T(8,128)(2,1)}), bf16[8,8,2048]{2,1,0:T(8,128)(2,1)S(1)}, u32[]{:S(2)}, u32[]{:S(2)}) async-start(bf16[8,8,2048]{2,1,0:T(8,128)(2,1)} %broadcast_in_dim.55), calls=%async_computation | async-start | bytes 524288 | tf_op jit(solution)/shard_map/all_to_all | solution.py:60
  25.3 14.2 %collective-permute-start.2 = (bf16[64,2048]{1,0:T(8,128)(2,1)S(1)}, bf16[64,2048]{1,0:T(8,128)(2,1)S(1)}, u32[]{:S(2)}, u32[]{:S(2)}) collective-permute-start(bf16[64,2048]{1,0:T(8,128)(2,1)S(1)} %bitcast.48), channel_id=1, source_target_pairs={{0,6},{2,0},{4,2},{6,4},{1,7},{3,1},{5,3},{7,5},{8,14},{10,8},{12,... | collective-permute-start | bytes 786440 | tf_op jit(solution)/shard_map/ppermute | solution.py:65
  25.8 15.1 %collective-permute-start.3 = (bf16[64,2048]{1,0:T(8,128)(2,1)S(1)}, bf16[64,2048]{1,0:T(8,128)(2,1)S(1)}, u32[]{:S(2)}, u32[]{:S(2)}) collective-permute-start(bf16[64,2048]{1,0:T(8,128)(2,1)S(1)} %bitcast.49), channel_id=1, source_target_pairs={{0,4},{2,6},{4,0},{6,2},{1,5},{3,7},{5,1},{7,3},{8,12},{10,14},{12... | collective-permute-start | bytes 786440 | tf_op jit(solution)/shard_map/ppermute | solution.py:65
  26.4 14.4 %collective-permute-start.4 = (bf16[64,2048]{1,0:T(8,128)(2,1)S(1)}, bf16[64,2048]{1,0:T(8,128)(2,1)S(1)}, u32[]{:S(2)}, u32[]{:S(2)}) collective-permute-start(bf16[64,2048]{1,0:T(8,128)(2,1)S(1)} %bitcast.50), channel_id=1, source_target_pairs={{0,2},{2,4},{4,6},{6,0},{1,3},{3,5},{5,7},{7,1},{8,10},{10,12},{12... | collective-permute-start | bytes 786440 | tf_op jit(solution)/shard_map/ppermute | solution.py:65
  29.8 12.2 %collective-permute-start.5 = (bf16[64,2048]{1,0:T(8,128)(2,1)S(1)}, bf16[64,2048]{1,0:T(8,128)(2,1)S(1)}, u32[]{:S(2)}, u32[]{:S(2)}) collective-permute-start(bf16[64,2048]{1,0:T(8,128)(2,1)S(1)} %bitcast.51), channel_id=1, source_target_pairs={{0,1},{1,0},{2,3},{3,2},{4,5},{5,4},{6,7},{7,6},{8,9},{9,8},{10,11... | collective-permute-start | bytes 786440 | tf_op jit(solution)/shard_map/ppermute | solution.py:29
  39.5 2.6 %collective-permute-start.6 = (bf16[64,2048]{1,0:T(8,128)(2,1)S(1)}, bf16[64,2048]{1,0:T(8,128)(2,1)S(1)}, u32[]{:S(2)}, u32[]{:S(2)}) collective-permute-start(bf16[64,2048]{1,0:T(8,128)(2,1)S(1)} %collective-permute-done.2), channel_id=1, source_target_pairs={{0,1},{1,0},{2,3},{3,2},{4,5},{5,4},{6,7},{7,6},{8,9},{9,8},{10,11... | collective-permute-start | bytes 786440 | tf_op jit(solution)/shard_map/ppermute | solution.py:29
  43.8 2.7 %collective-permute-start.9 = (bf16[256,2048]{1,0:T(8,128)(2,1)S(1)}, bf16[256,2048]{1,0:T(8,128)(2,1)S(1)}, u32[]{:S(2)}, u32[]{:S(2)}) collective-permute-start(bf16[256,2048]{1,0:T(8,128)(2,1)S(1)} %convolution_convert_fusion), channel_id=1, source_target_pairs={{0,1},{1,0},{2,3},{3,2},{4,5},{5,4},{6,7},{7,6},{8,9},{9,8},{10,11... | collective-permute-start | bytes 3145736 | tf_op jit(solution)/shard_map/ppermute | solution.py:29
  46.8 8.1 %collective-permute-start.10 = (bf16[64,2048]{1,0:T(8,128)(2,1)S(1)}, bf16[64,2048]{1,0:T(8,128)(2,1)S(1)}, u32[]{:S(2)}, u32[]{:S(2)}) collective-permute-start(bf16[64,2048]{1,0:T(8,128)(2,1)S(1)} %get-tuple-element.23), channel_id=1, source_target_pairs={{0,2},{2,4},{4,6},{6,0},{1,3},{3,5},{5,7},{7,1},{8,10},{10,12},{12... | collective-permute-start | bytes 786440 | tf_op jit(solution)/shard_map/ppermute | solution.py:65
  49.1 8.8 %collective-permute-start.11 = (bf16[64,2048]{1,0:T(8,128)(2,1)S(1)}, bf16[64,2048]{1,0:T(8,128)(2,1)S(1)}, u32[]{:S(2)}, u32[]{:S(2)}) collective-permute-start(bf16[64,2048]{1,0:T(8,128)(2,1)S(1)} %get-tuple-element.25), channel_id=1, source_target_pairs={{0,4},{2,6},{4,0},{6,2},{1,5},{3,7},{5,1},{7,3},{8,12},{10,14},{12... | collective-permute-start | bytes 786440 | tf_op jit(solution)/shard_map/ppermute | solution.py:65
  49.1 14.8 %collective-permute-start.12 = (bf16[64,2048]{1,0:T(8,128)(2,1)S(1)}, bf16[64,2048]{1,0:T(8,128)(2,1)S(1)}, u32[]{:S(2)}, u32[]{:S(2)}) collective-permute-start(bf16[64,2048]{1,0:T(8,128)(2,1)S(1)} %get-tuple-element.24), channel_id=1, source_target_pairs={{0,6},{2,0},{4,2},{6,4},{1,7},{3,1},{5,3},{7,5},{8,14},{10,8},{12,... | collective-permute-start | bytes 786440 | tf_op jit(solution)/shard_map/ppermute | solution.py:65
  64.7 14.1 %all-to-all-start.1 = ((bf16[8,8,2048]{2,1,0:T(8,128)(2,1)}), bf16[8,8,2048]{2,1,0:T(8,128)(2,1)S(1)}, u32[]{:S(2)}, u32[]{:S(2)}) async-start(bf16[8,8,2048]{2,1,0:T(8,128)(2,1)} %fusion.28), calls=%async_computation.1 | async-start | bytes 524288 | tf_op jit(solution)/shard_map/all_to_all | solution.py:60
  68.1 10.7 %collective-permute-start = (bf16[4,2048]{1,0:T(4,128)(2,1)S(1)}, bf16[4,2048]{1,0:T(4,128)(2,1)S(1)}, u32[]{:S(2)}, u32[]{:S(2)}) collective-permute-start(bf16[4,2048]{1,0:T(4,128)(2,1)S(1)} %get-tuple-element.30), channel_id=1, source_target_pairs={{0,1},{1,0},{2,3},{3,2},{4,5},{5,4},{6,7},{7,6},{8,9},{9,8},{10,11... | collective-permute-start | bytes 49160 | tf_op jit(solution)/shard_map/ppermute | solution.py:29
  79.0 3.0 %collective-permute-start.13 = (f32[8,1]{0,1:T(1,128)S(1)}, f32[8,1]{0,1:T(1,128)S(1)}, u32[]{:S(2)}, u32[]{:S(2)}) collective-permute-start(f32[8,1]{0,1:T(1,128)S(1)} %bitcast.60), channel_id=1, source_target_pairs={{0,1},{1,0},{2,3},{3,2},{4,5},{5,4},{6,7},{7,6},{8,9},{9,8},{10,11... | collective-permute-start | bytes 104 | tf_op jit(solution)/shard_map/ppermute | solution.py:29
  82.8 15.7 %all-to-all-start.2 = ((bf16[8,8,2048]{2,1,0:T(8,128)(2,1)}), bf16[8,8,2048]{2,1,0:T(8,128)(2,1)S(1)}, u32[]{:S(2)}, u32[]{:S(2)}) async-start(bf16[8,8,2048]{2,1,0:T(8,128)(2,1)} %broadcast_in_dim.57), calls=%async_computation.2 | async-start | bytes 524288 | tf_op jit(solution)/shard_map/all_to_all | solution.py:60
  98.5 14.2 %collective-permute-start.14 = (bf16[64,2048]{1,0:T(8,128)(2,1)S(1)}, bf16[64,2048]{1,0:T(8,128)(2,1)S(1)}, u32[]{:S(2)}, u32[]{:S(2)}) collective-permute-start(bf16[64,2048]{1,0:T(8,128)(2,1)S(1)} %bitcast.43), channel_id=1, source_target_pairs={{0,6},{2,0},{4,2},{6,4},{1,7},{3,1},{5,3},{7,5},{8,14},{10,8},{12,... | collective-permute-start | bytes 786440 | tf_op jit(solution)/shard_map/ppermute | solution.py:65
  98.5 14.2 %collective-permute-start.15 = (bf16[64,2048]{1,0:T(8,128)(2,1)S(1)}, bf16[64,2048]{1,0:T(8,128)(2,1)S(1)}, u32[]{:S(2)}, u32[]{:S(2)}) collective-permute-start(bf16[64,2048]{1,0:T(8,128)(2,1)S(1)} %bitcast.44), channel_id=1, source_target_pairs={{0,4},{2,6},{4,0},{6,2},{1,5},{3,7},{5,1},{7,3},{8,12},{10,14},{12... | collective-permute-start | bytes 786440 | tf_op jit(solution)/shard_map/ppermute | solution.py:65
  99.8 13.3 %collective-permute-start.16 = (bf16[64,2048]{1,0:T(8,128)(2,1)S(1)}, bf16[64,2048]{1,0:T(8,128)(2,1)S(1)}, u32[]{:S(2)}, u32[]{:S(2)}) collective-permute-start(bf16[64,2048]{1,0:T(8,128)(2,1)S(1)} %bitcast.45), channel_id=1, source_target_pairs={{0,2},{2,4},{4,6},{6,0},{1,3},{3,5},{5,7},{7,1},{8,10},{10,12},{12... | collective-permute-start | bytes 786440 | tf_op jit(solution)/shard_map/ppermute | solution.py:65
  101.3 17.6 %collective-permute-start.17 = (bf16[64,2048]{1,0:T(8,128)(2,1)S(1)}, bf16[64,2048]{1,0:T(8,128)(2,1)S(1)}, u32[]{:S(2)}, u32[]{:S(2)}) collective-permute-start(bf16[64,2048]{1,0:T(8,128)(2,1)S(1)} %bitcast.46), channel_id=1, source_target_pairs={{0,1},{1,0},{2,3},{3,2},{4,5},{5,4},{6,7},{7,6},{8,9},{9,8},{10,11... | collective-permute-start | bytes 786440 | tf_op jit(solution)/shard_map/ppermute | solution.py:29
  113.2 5.8 %collective-permute-start.18 = (bf16[64,2048]{1,0:T(8,128)(2,1)S(1)}, bf16[64,2048]{1,0:T(8,128)(2,1)S(1)}, u32[]{:S(2)}, u32[]{:S(2)}) collective-permute-start(bf16[64,2048]{1,0:T(8,128)(2,1)S(1)} %collective-permute-done.14), channel_id=1, source_target_pairs={{0,1},{1,0},{2,3},{3,2},{4,5},{5,4},{6,7},{7,6},{8,9},{9,8},{10,11... | collective-permute-start | bytes 786440 | tf_op jit(solution)/shard_map/ppermute | solution.py:29
  114.8 4.2 %collective-permute-start.19 = (bf16[64,2048]{1,0:T(8,128)(2,1)S(1)}, bf16[64,2048]{1,0:T(8,128)(2,1)S(1)}, u32[]{:S(2)}, u32[]{:S(2)}) collective-permute-start(bf16[64,2048]{1,0:T(8,128)(2,1)S(1)} %collective-permute-done.15), channel_id=1, source_target_pairs={{0,1},{1,0},{2,3},{3,2},{4,5},{5,4},{6,7},{7,6},{8,9},{9,8},{10,11... | collective-permute-start | bytes 786440 | tf_op jit(solution)/shard_map/ppermute | solution.py:29
  114.9 4.1 %collective-permute-start.20 = (bf16[64,2048]{1,0:T(8,128)(2,1)S(1)}, bf16[64,2048]{1,0:T(8,128)(2,1)S(1)}, u32[]{:S(2)}, u32[]{:S(2)}) collective-permute-start(bf16[64,2048]{1,0:T(8,128)(2,1)S(1)} %collective-permute-done.16), channel_id=1, source_target_pairs={{0,1},{1,0},{2,3},{3,2},{4,5},{5,4},{6,7},{7,6},{8,9},{9,8},{10,11... | collective-permute-start | bytes 786440 | tf_op jit(solution)/shard_map/ppermute | solution.py:29
  121.9 4.0 %collective-permute-start.21 = (f32[8,128]{1,0:T(8,128)S(1)}, f32[8,128]{1,0:T(8,128)S(1)}, u32[]{:S(2)}, u32[]{:S(2)}) collective-permute-start(f32[8,128]{1,0:T(8,128)S(1)} %bitcast.55), channel_id=1, source_target_pairs={{0,128},{64,192},{128,0},{192,64},{1,129},{65,193},{129,1},{193,65... | collective-permute-start | bytes 12296 | tf_op jit(solution)/shard_map/ppermute | solution.py:157
  123.1 2.8 %collective-permute-start.22 = (f32[8,128]{1,0:T(8,128)S(1)}, f32[8,128]{1,0:T(8,128)S(1)}, u32[]{:S(2)}, u32[]{:S(2)}) collective-permute-start(f32[8,128]{1,0:T(8,128)S(1)} %bitcast.56), channel_id=1, source_target_pairs={{0,64},{64,128},{128,192},{192,0},{1,65},{65,129},{129,193},{193,1... | collective-permute-start | bytes 12296 | tf_op jit(solution)/shard_map/ppermute | solution.py:157
  124.9 3.7 %collective-permute-start.23 = (f32[8,128]{1,0:T(8,128)S(1)}, f32[8,128]{1,0:T(8,128)S(1)}, u32[]{:S(2)}, u32[]{:S(2)}) collective-permute-start(f32[8,128]{1,0:T(8,128)S(1)} %bitcast.57), channel_id=1, source_target_pairs={{0,192},{64,0},{128,64},{192,128},{1,193},{65,1},{129,65},{193,129... | collective-permute-start | bytes 12296 | tf_op jit(solution)/shard_map/ppermute | solution.py:157
  129.2 16.2 %all-to-all-start.3 = ((f32[64,2,128]{2,1,0:T(2,128)}), f32[64,2,128]{2,1,0:T(2,128)S(1)}, u32[]{:S(2)}, u32[]{:S(2)}) async-start(f32[64,2,128]{2,1,0:T(2,128)} %broadcast_in_dim.58), calls=%async_computation.3 | async-start | bytes 131072 | tf_op jit(solution)/shard_map/all_to_all | solution.py:60
  150.7 2.8 %collective-permute-start.25 = (bf16[256,2048]{1,0:T(8,128)(2,1)S(1)}, bf16[256,2048]{1,0:T(8,128)(2,1)S(1)}, u32[]{:S(2)}, u32[]{:S(2)}) collective-permute-start(bf16[256,2048]{1,0:T(8,128)(2,1)S(1)} %convolution_convert_fusion.1), channel_id=1, source_target_pairs={{0,1},{1,0},{2,3},{3,2},{4,5},{5,4},{6,7},{7,6},{8,9},{9,8},{10,11... | collective-permute-start | bytes 3145736 | tf_op jit(solution)/shard_map/ppermute | solution.py:29
  153.7 7.8 %collective-permute-start.26 = (bf16[64,2048]{1,0:T(8,128)(2,1)S(1)}, bf16[64,2048]{1,0:T(8,128)(2,1)S(1)}, u32[]{:S(2)}, u32[]{:S(2)}) collective-permute-start(bf16[64,2048]{1,0:T(8,128)(2,1)S(1)} %get-tuple-element.20), channel_id=1, source_target_pairs={{0,2},{2,4},{4,6},{6,0},{1,3},{3,5},{5,7},{7,1},{8,10},{10,12},{12... | collective-permute-start | bytes 786440 | tf_op jit(solution)/shard_map/ppermute | solution.py:65
  155.8 8.8 %collective-permute-start.27 = (bf16[64,2048]{1,0:T(8,128)(2,1)S(1)}, bf16[64,2048]{1,0:T(8,128)(2,1)S(1)}, u32[]{:S(2)}, u32[]{:S(2)}) collective-permute-start(bf16[64,2048]{1,0:T(8,128)(2,1)S(1)} %get-tuple-element.22), channel_id=1, source_target_pairs={{0,4},{2,6},{4,0},{6,2},{1,5},{3,7},{5,1},{7,3},{8,12},{10,14},{12... | collective-permute-start | bytes 786440 | tf_op jit(solution)/shard_map/ppermute | solution.py:65
  156.3 14.9 %collective-permute-start.28 = (bf16[64,2048]{1,0:T(8,128)(2,1)S(1)}, bf16[64,2048]{1,0:T(8,128)(2,1)S(1)}, u32[]{:S(2)}, u32[]{:S(2)}) collective-permute-start(bf16[64,2048]{1,0:T(8,128)(2,1)S(1)} %get-tuple-element.21), channel_id=1, source_target_pairs={{0,6},{2,0},{4,2},{6,4},{1,7},{3,1},{5,3},{7,5},{8,14},{10,8},{12,... | collective-permute-start | bytes 786440 | tf_op jit(solution)/shard_map/ppermute | solution.py:65
  172.0 15.2 %all-to-all-start.4 = ((bf16[8,8,2048]{2,1,0:T(8,128)(2,1)}), bf16[8,8,2048]{2,1,0:T(8,128)(2,1)S(1)}, u32[]{:S(2)}, u32[]{:S(2)}) async-start(bf16[8,8,2048]{2,1,0:T(8,128)(2,1)} %fusion.29), calls=%async_computation.4 | async-start | bytes 524288 | tf_op jit(solution)/shard_map/all_to_all | solution.py:60
  175.4 14.2 %collective-permute-start.24 = (f32[4,2048]{1,0:T(4,128)S(1)}, f32[4,2048]{1,0:T(4,128)S(1)}, u32[]{:S(2)}, u32[]{:S(2)}) collective-permute-start(f32[4,2048]{1,0:T(4,128)S(1)} %get-tuple-element.28), channel_id=1, source_target_pairs={{0,1},{1,0},{2,3},{3,2},{4,5},{5,4},{6,7},{7,6},{8,9},{9,8},{10,11... | collective-permute-start | bytes 98312 | tf_op jit(solution)/shard_map/ppermute | solution.py:29
  187.2 2.4 %collective-permute-start.29 = (f32[4,2048]{1,0:T(4,128)S(1)}, f32[4,2048]{1,0:T(4,128)S(1)}, u32[]{:S(2)}, u32[]{:S(2)}) collective-permute-start(f32[4,2048]{1,0:T(4,128)S(1)} %get-tuple-element.26), channel_id=1, source_target_pairs={{0,1},{1,0},{2,3},{3,2},{4,5},{5,4},{6,7},{7,6},{8,9},{9,8},{10,11... | collective-permute-start | bytes 98312 | tf_op jit(solution)/shard_map/ppermute | solution.py:29
  (10 other events, 139.5 us)
